TPU v7x, 32 devices: a whole 2x2x4 slice. The times are simulated.
32 devices in a mesh: seq: 8 (over y, x, core), head: 4 (over z).
Axes of the slice: x: 2, y: 2, z: 4, core: 2. Of those that a mesh axis runs over, the one named last changes fastest.
Arguments:
- queries: bfloat16 [8192, 4096], P(('seq', 'head')), may hold values from -40 to 40
- keys: bfloat16 [8192, 4096], P(('seq', 'head')), may hold values from -4 to 4
- values: bfloat16 [8192, 4096], P(('seq', 'head')), may hold values from -40 to 40
- grad_out: bfloat16 [8192, 4096], P(('seq', 'head')), may hold values from -40 to 40
Outputs:
- output: bfloat16 [8192, 4096], P(('seq', 'head'))
- grad_queries: bfloat16 [8192, 4096], P(('seq', 'head'))
- grad_keys: bfloat16 [8192, 4096], P(('seq', 'head'))
- grad_values: bfloat16 [8192, 4096], P(('seq', 'head'))
All inputs are finite; a program needn't handle non-finite values.
Results may differ from a plain program's by a relative error of at most 0.01.
Values may be sent and summed in bfloat16 or wider, within the bound.
No kernel may reach another device: no remote copies, remote signals or barrier semaphores. Data moves between devices by JAX's collectives and lax.ppermute only.
A program may use at most 128 MiB of HBM per device.

v0:
```python
import jax
import jax.numpy as jnp
from jax import lax
from jax.sharding import PartitionSpec as P

HEADS = 32
DH = 128


epsilon = 1e-06


def carried_in(part, axis, combine, identity):
    place = lax.axis_index(axis)
    gathered = lax.all_gather(part, axis)
    state = jnp.zeros_like(part) + jnp.asarray(identity, part.dtype)

    def carried_one(step, state):
        return combine(state, lax.dynamic_index_in_dim(gathered, step, 0, False))

    return lax.fori_loop(0, place, carried_one, state)


def prefix(shard, axis, join, neutral):
    count = lax.axis_size(axis)
    place = lax.axis_index(axis)
    ahead = count - 1 - place
    gathered = lax.all_gather(shard.astype(jnp.bfloat16), axis)
    state = jnp.zeros_like(shard) + jnp.asarray(neutral, shard.dtype)

    def prefix_one(step, state):
        source = count - 1 - step
        return join(state, lax.dynamic_index_in_dim(gathered, source, 0, False).astype(shard.dtype))

    return lax.fori_loop(0, ahead, prefix_one, state)


def feature_map(x):
    xf = x.astype(jnp.float32)
    return jnp.where(xf > 0, xf + 1.0, jnp.exp(jnp.minimum(xf, 0.0)))


def feature_slope(x):
    xf = x.astype(jnp.float32)
    return jnp.where(xf > 0, 1.0, jnp.exp(jnp.minimum(xf, 0.0)))


def add_states(earlier, later):
    return earlier + later


def local(queries, keys, values, grad_out):
    groups = lax.axis_size("head")
    heads_local = HEADS // groups
    query_head, key_head, value_head, grad_head = (
        lax.all_to_all(queries, "head", split_axis=1, concat_axis=0, tiled=True),
        lax.all_to_all(keys, "head", split_axis=1, concat_axis=0, tiled=True),
        lax.all_to_all(values, "head", split_axis=1, concat_axis=0, tiled=True),
        lax.all_to_all(grad_out, "head", split_axis=1, concat_axis=0, tiled=True),
    )
    tok_rows = query_head.shape[0]
    shape3 = (tok_rows, heads_local, DH)
    query_raw = query_head.reshape(shape3)
    key_raw = key_head.reshape(shape3)
    value_in = value_head.reshape(shape3)
    grad_norm = grad_head.reshape(shape3).astype(jnp.float32)
    query_feat = feature_map(query_raw).astype(jnp.bfloat16)
    key_feat = feature_map(key_raw).astype(jnp.bfloat16)
    own_state = jnp.einsum("shd,she->hde", key_feat, value_in, preferred_element_type=jnp.float32)
    empty_state = jnp.zeros((heads_local, DH, DH), jnp.float32)
    prefix_state = carried_in(own_state, "seq", add_states, empty_state)
    prefix_bf = prefix_state.astype(jnp.bfloat16)
    causal = (jnp.arange(tok_rows)[:, None] >= jnp.arange(tok_rows)[None, :])[None]
    scores = jnp.einsum("thd,shd->hts", query_feat, key_feat, preferred_element_type=jnp.float32)
    scores = jnp.where(causal, scores, 0.0).astype(jnp.bfloat16)
    mixed = jnp.einsum("hts,she->the", scores, value_in, preferred_element_type=jnp.float32)
    mixed = mixed + jnp.einsum(
        "thd,hde->the", query_feat, prefix_bf, preferred_element_type=jnp.float32
    )
    inv_rms = lax.rsqrt(jnp.mean(mixed * mixed, -1, keepdims=True) + epsilon)
    normed = mixed * inv_rms
    output_head = normed.astype(jnp.bfloat16).reshape(tok_rows, heads_local * DH)
    output = lax.all_to_all(output_head, "head", split_axis=0, concat_axis=1, tiled=True)
    grad_mix = inv_rms * (grad_norm - normed * jnp.mean(grad_norm * normed, -1, keepdims=True))
    grad_mix = grad_mix.astype(jnp.bfloat16)
    query_grad_state = jnp.einsum(
        "thd,the->hde", query_feat, grad_mix, preferred_element_type=jnp.float32
    )
    suffix_state = prefix(query_grad_state, "seq", add_states, empty_state)
    suffix_bf = suffix_state.astype(jnp.bfloat16)
    grad_scores = jnp.einsum("the,she->hts", grad_mix, value_in, preferred_element_type=jnp.float32)
    grad_scores = jnp.where(causal, grad_scores, 0.0).astype(jnp.bfloat16)
    grad_qf = jnp.einsum("the,hde->thd", grad_mix, prefix_bf, preferred_element_type=jnp.float32)
    grad_qf = grad_qf + jnp.einsum(
        "hts,shd->thd", grad_scores, key_feat, preferred_element_type=jnp.float32
    )
    grad_kf = jnp.einsum("she,hde->shd", value_in, suffix_bf, preferred_element_type=jnp.float32)
    grad_kf = grad_kf + jnp.einsum(
        "hts,thd->shd", grad_scores, query_feat, preferred_element_type=jnp.float32
    )
    grad_vf = jnp.einsum("shd,hde->she", key_feat, suffix_bf, preferred_element_type=jnp.float32)
    grad_vf = grad_vf + jnp.einsum(
        "hts,the->she", scores, grad_mix, preferred_element_type=jnp.float32
    )
    flat_shape = (tok_rows, heads_local * DH)
    grad_q = (grad_qf * feature_slope(query_raw)).astype(jnp.bfloat16).reshape(flat_shape)
    grad_k = (grad_kf * feature_slope(key_raw)).astype(jnp.bfloat16).reshape(flat_shape)
    grad_v = grad_vf.astype(jnp.bfloat16).reshape(flat_shape)
    grad_queries, grad_keys, grad_values = (
        lax.all_to_all(grad_q, "head", split_axis=0, concat_axis=1, tiled=True),
        lax.all_to_all(grad_k, "head", split_axis=0, concat_axis=1, tiled=True),
        lax.all_to_all(grad_v, "head", split_axis=0, concat_axis=1, tiled=True),
    )
    return (output, grad_queries, grad_keys, grad_values)


def solution(mesh):
    placed = (
        P(("seq", "head"), None),
        P(("seq", "head"), None),
        P(("seq", "head"), None),
        P(("seq", "head"), None),
    )
    return jax.shard_map(
        local,
        mesh=mesh,
        in_specs=placed,
        out_specs=(
            P(("seq", "head"), None),
            P(("seq", "head"), None),
            P(("seq", "head"), None),
            P(("seq", "head"), None),
        ),
        check_vma=False,
    )
```

profile of v0, /device:TPU:6, one launch (start us, length us, event | category | flops | bytes accessed | tf_op | source)
XLA Modules:
  0.0 538.3 jit_solution(9816396691735333648)
XLA Ops:
  10.3 4.9 all-to-all-start.1
  15.2 4.1 copy.58
  19.2 44.1 %all-to-all-done.1 = bf16[256,4,1024]{2,0,1:T(8,128)(2,1)S(1)} async-done(((bf16[256,4,1024]{2,0,1:T(8,128)(2,1)}), bf16[256,4,1024]{2,0,1:T(8,128)(2,1)S(1)}, u32[]{:S(2)}, u32[]{:S(2)}) %all-to-all-start.1) | async-done | bytes 2097184 | tf_op jit(solution)/shard_map/all_to_all | solution.py:57
  64.7 3.6 all-to-all-start.2
  71.4 44.6 %all-to-all-done.2 = bf16[256,4,1024]{0,2,1:T(8,128)(2,1)S(1)} async-done(((bf16[256,4,1024]{0,2,1:T(8,128)(2,1)}), bf16[256,4,1024]{0,2,1:T(8,128)(2,1)S(1)}, u32[]{:S(2)}, u32[]{:S(2)}) %all-to-all-start.2) | async-done | bytes 2097184 | tf_op jit(solution)/shard_map/all_to_all | solution.py:58
  116.0 4.5 all-to-all-start
  120.6 4.8 fusion.7
  130.3 3.2 reshape.102
  133.5 4.2 copy.60
  140.8 4.1 copy.65
  144.9 23.4 %all-to-all-done = bf16[256,4,1024]{2,0,1:T(8,128)(2,1)} async-done(((bf16[256,4,1024]{2,0,1:T(8,128)(2,1)}), bf16[256,4,1024]{2,0,1:T(8,128)(2,1)}, u32[]{:S(2)}, u32[]{:S(2)}) %all-to-all-start) | async-done | bytes 2097184 | tf_op jit(solution)/shard_map/all_to_all | solution.py:56
  168.3 4.7 all-to-all-start.4
  173.3 5.2 fusion.3
  180.5 4.1 copy.73
  184.6 36.2 %all-to-all-done.4 = bf16[256,4,1024]{0,2,1:T(8,128)(2,1)} async-done(((bf16[256,4,1024]{0,2,1:T(8,128)(2,1)}), bf16[256,4,1024]{0,2,1:T(8,128)(2,1)}, u32[]{:S(2)}, u32[]{:S(2)}) %all-to-all-start.4) | async-done | bytes 2097184 | tf_op jit(solution)/shard_map/all_to_all | solution.py:59
  222.7 4.7 copy.66
  227.4 5.9 %reshape.104 = f32[1024,8,128]{0,2,1:T(8,128)} reshape(f32[4,256,1024]{1,0,2:T(4,128)} %copy.66) | data formatting | bytes 8388608 | tf_op jit(solution)/shard_map/convert_element_type | solution.py:66
  233.3 5.2 copy.100
  238.5 5.4 %copy.94 = f32[1024,8,128]{0,2,1:T(8,128)} copy(f32[1024,8,128]{2,1,0:T(8,128)} %bitcast.101) | data formatting | bytes 8388608 | tf_op jit(solution)/shard_map/jit(_where)/select_n | solution.py:45
  243.9 10.5 %select_convert_fusion.1 = bf16[8,1024,1024]{2,1,0:T(8,128)(2,1)} fusion(pred[1024,1024]{1,0:T(8,128)(4,1)S(1)} %iota_compare_fusion, bf16[1024,8,128]{0,2,1:T(8,128)(2,1)} %copy.73, bf16[1024,8,128]{2,1,0:T(8,128)(2,1)} %bitcast.97), kind=kOutput, calls=%fused_computation.3 | convolution fusion | flops 2164260864 | bytes 22020096 | tf_op jit(solution)/shard_map/thd,shd->hts/dot_general | solution.py:74
  254.4 11.4 %fusion.19 = f32[8,1024,128]{1,2,0:T(8,128)} fusion(bf16[8,1024,1024]{2,1,0:T(8,128)(2,1)} %select_convert_fusion.1, bf16[1024,8,128]{0,2,1:T(8,128)(2,1)S(1)} %reshape.102), kind=kOutput, calls=%fused_computation.42 | convolution fusion | flops 2147483648 | bytes 23068672 | tf_op jit(solution)/shard_map/hts,she->the/dot_general | solution.py:76
  265.8 7.2 %while.22 = (s32[]{:T(128)}, f32[8,128,128]{2,1,0:T(8,128)S(1)}, s32[]{:T(128)}, f32[8,8,128,128]{3,2,1,0:T(8,128)}, s32[]{:T(128)}, /*index=5*/s32[]{:T(128)}, s32[]{:T(128)}) while((s32[]{:T(128)}, f32[8,128,128]{2,1,0:T(8,128)S(1)}, s32[]{:T(128)}, f32[8,8,128,128]{3,2,1,0:T(8,128)}, s32[]{:T(128)}, /*index=5*/s32[]{:T(128)}, ...), condition=%wide.region_1.2_spmd, body=%wide.region_0.1_spmd.sunk | while | flops 131077 | bytes 1572979 | solution.py:21
  273.0 3.8 multiply_reduce_fusion.1
  282.2 8.5 %select_convert_fusion = bf16[8,1024,1024]{2,1,0:T(8,128)(2,1)} fusion(pred[1024,1024]{1,0:T(8,128)(4,1)S(1)} %copy-done.5, bf16[1024,8,128]{0,2,1:T(8,128)(2,1)S(1)} %get-tuple-element.105, bf16[1024,8,128]{0,2,1:T(8,128)(2,1)S(1)} %reshape.102), kind=kOutput, calls=%fused_computation.2 | convolution fusion | flops 2164260864 | bytes 22020096 | tf_op jit(solution)/shard_map/the,she->hts/dot_general | solution.py:91
  290.7 14.0 %fusion.21 = f32[8,128,1024]{2,1,0:T(8,128)} fusion(bf16[1024,8,128]{0,2,1:T(8,128)(2,1)} %copy.60, bf16[8,1024,1024]{2,1,0:T(8,128)(2,1)} %select_convert_fusion), kind=kOutput, calls=%fused_computation.44 | convolution fusion | flops 2147483648 | bytes 23068672 | tf_op jit(solution)/shard_map/hts,shd->thd/dot_general | solution.py:94
  304.8 6.1 %fusion.9 = bf16[1024,8,128]{0,2,1:T(8,128)(2,1)} fusion(f32[1024,8,128]{0,2,1:T(8,128)} %copy.94, f32[8,128,1024]{2,1,0:T(8,128)} %fusion.21, bf16[1024,8,128]{0,2,1:T(8,128)(2,1)} %copy-done.1, f32[8,128,128]{2,1,0:T(8,128)S(1)} %get-tuple-element.83), kind=kOutput, calls=%fused_computation.21 | convolution fusion | flops 271712256 | bytes 13107200 | tf_op jit(solution)/shard_map/the,hde->thd/dot_general | solution.py:93
  310.9 4.5 all_to_all.111
  318.6 4.4 all-to-all-start.5
  323.1 3.6 convolution_convert_fusion
  326.7 4.5 all_to_all.105
  334.4 37.6 %all-to-all-done.5 = bf16[4,256,1024]{1,2,0:T(8,128)(2,1)} async-done(((bf16[4,256,1024]{1,2,0:T(8,128)(2,1)}), bf16[4,256,1024]{1,2,0:T(8,128)(2,1)}, u32[]{:S(2)}, u32[]{:S(2)}) %all-to-all-start.5) | async-done | bytes 2097184 | tf_op jit(solution)/shard_map/all_to_all | solution.py:110
  372.1 4.6 all-to-all-start.3
  376.7 10.8 %fusion.23 = f32[8,128,1024]{2,1,0:T(8,128)} fusion(bf16[1024,8,128]{0,2,1:T(8,128)(2,1)} %copy-done.1, bf16[8,1024,1024]{2,1,0:T(8,128)(2,1)} %select_convert_fusion.1), kind=kOutput, calls=%fused_computation.46 | convolution fusion | flops 2147483648 | bytes 23068672 | tf_op jit(solution)/shard_map/hts,the->she/dot_general | solution.py:102
  388.6 5.1 fusion.12
  393.7 4.5 all_to_all.119
  398.2 3.2 copy.81
  401.4 23.4 %all-to-all-done.3 = bf16[4,256,1024]{1,2,0:T(8,128)(2,1)} async-done(((bf16[4,256,1024]{1,2,0:T(8,128)(2,1)}), bf16[4,256,1024]{1,2,0:T(8,128)(2,1)}, u32[]{:S(2)}, u32[]{:S(2)}) %all-to-all-start.3) | async-done | bytes 2097184 | tf_op jit(solution)/shard_map/all_to_all | solution.py:83
  424.8 4.5 all-to-all-start.7
  429.3 5.1 copy.101
  434.4 5.4 %copy.95 = f32[1024,8,128]{0,2,1:T(8,128)} copy(f32[1024,8,128]{2,1,0:T(8,128)} %bitcast.102) | data formatting | bytes 8388608 | tf_op jit(solution)/shard_map/jit(_where)/select_n | solution.py:45
  439.9 8.9 %fusion.22 = f32[8,128,1024]{2,1,0:T(8,128)S(1)} fusion(bf16[1024,8,128]{0,2,1:T(8,128)(2,1)} %copy.73, bf16[8,1024,1024]{2,1,0:T(8,128)(2,1)} %select_convert_fusion), kind=kOutput, calls=%fused_computation.45 | convolution fusion | flops 2147483648 | bytes 23068672 | tf_op jit(solution)/shard_map/hts,thd->shd/dot_general | solution.py:98
  450.9 3.3 all_to_all.115
  455.8 21.3 %all-to-all-done.7 = bf16[4,256,1024]{1,2,0:T(8,128)(2,1)} async-done(((bf16[4,256,1024]{1,2,0:T(8,128)(2,1)}), bf16[4,256,1024]{1,2,0:T(8,128)(2,1)}, u32[]{:S(2)}, u32[]{:S(2)}) %all-to-all-start.7) | async-done | bytes 2097184 | tf_op jit(solution)/shard_map/all_to_all | solution.py:112
  477.1 3.6 all-to-all-start.6
  480.7 4.1 copy.83
  484.8 4.1 copy.82
  488.9 4.1 copy.85
  493.0 35.5 %all-to-all-done.6 = bf16[4,256,1024]{1,2,0:T(8,128)(2,1)S(1)} async-done(((bf16[4,256,1024]{1,2,0:T(8,128)(2,1)}), bf16[4,256,1024]{1,2,0:T(8,128)(2,1)S(1)}, u32[]{:S(2)}, u32[]{:S(2)}) %all-to-all-start.6) | async-done | bytes 2097184 | tf_op jit(solution)/shard_map/all_to_all | solution.py:111
  (45 shorter events, 47.3 us)
Async XLA Ops:
  10.3 53.1 %all-to-all-start.1 = ((bf16[256,4,1024]{2,0,1:T(8,128)(2,1)}), bf16[256,4,1024]{2,0,1:T(8,128)(2,1)S(1)}, u32[]{:S(2)}, u32[]{:S(2)}) async-start(bf16[256,4,1024]{2,0,1:T(8,128)(2,1)} %bitcast.90), calls=%async_computation.1 | async-start | bytes 4194304 | tf_op jit(solution)/shard_map/all_to_all | solution.py:57
  63.4 1.3 copy-start.3
  64.7 51.3 %all-to-all-start.2 = ((bf16[256,4,1024]{0,2,1:T(8,128)(2,1)}), bf16[256,4,1024]{0,2,1:T(8,128)(2,1)S(1)}, u32[]{:S(2)}, u32[]{:S(2)}) async-start(bf16[256,4,1024]{0,2,1:T(8,128)(2,1)} %bitcast.106), calls=%async_computation.2 | async-start | bytes 4194304 | tf_op jit(solution)/shard_map/all_to_all | solution.py:58
  116.0 52.3 %all-to-all-start = ((bf16[256,4,1024]{2,0,1:T(8,128)(2,1)}), bf16[256,4,1024]{2,0,1:T(8,128)(2,1)}, u32[]{:S(2)}, u32[]{:S(2)}) async-start(bf16[256,4,1024]{2,0,1:T(8,128)(2,1)} %bitcast.91), calls=%async_computation | async-start | bytes 4194304 | tf_op jit(solution)/shard_map/all_to_all | solution.py:56
  120.5 145.3 %all-gather.5.cloned.1.call-start = ((), (), s32[]{:S(2)}) async-start(), calls=%async_computation.8 | async-start | bytes 4718592 | tf_op jit(solution)/shard_map/all_gather | solution.py:15
  168.3 52.5 %all-to-all-start.4 = ((bf16[256,4,1024]{0,2,1:T(8,128)(2,1)}), bf16[256,4,1024]{0,2,1:T(8,128)(2,1)}, u32[]{:S(2)}, u32[]{:S(2)}) async-start(bf16[256,4,1024]{0,2,1:T(8,128)(2,1)} %bitcast.103), calls=%async_computation.4 | async-start | bytes 4194304 | tf_op jit(solution)/shard_map/all_to_all | solution.py:59
  173.3 70.6 %copy-start.4 = (pred[1024,1024]{1,0:T(8,128)(4,1)}, pred[1024,1024]{1,0:T(8,128)(4,1)S(1)}, u32[]{:S(2)}) copy-start(pred[1024,1024]{1,0:T(8,128)(4,1)S(1)} %iota_compare_fusion) | copy-start | bytes 3145732
  273.0 4.0 copy-start
  278.2 4.0 copy-start.5
  280.9 1.3 copy-start.1
  318.6 53.5 %all-to-all-start.5 = ((bf16[4,256,1024]{1,2,0:T(8,128)(2,1)}), bf16[4,256,1024]{1,2,0:T(8,128)(2,1)}, u32[]{:S(2)}, u32[]{:S(2)}) async-start(bf16[4,256,1024]{1,2,0:T(8,128)(2,1)} %copy.72), calls=%async_computation.5 | async-start | bytes 4194304 | tf_op jit(solution)/shard_map/all_to_all | solution.py:110
  323.0 64.4 %all-gather.7.cloned.1.call-start = ((), (), s32[]{:S(2)}) async-start(), calls=%async_computation.9 | async-start | bytes 2359296 | tf_op jit(solution)/shard_map/all_gather | solution.py:28
  372.1 52.8 %all-to-all-start.3 = ((bf16[4,256,1024]{1,2,0:T(8,128)(2,1)}), bf16[4,256,1024]{1,2,0:T(8,128)(2,1)}, u32[]{:S(2)}, u32[]{:S(2)}) async-start(bf16[4,256,1024]{1,2,0:T(8,128)(2,1)} %copy.64), calls=%async_computation.3 | async-start | bytes 4194304 | tf_op jit(solution)/shard_map/all_to_all | solution.py:83
  424.8 52.3 %all-to-all-start.7 = ((bf16[4,256,1024]{1,2,0:T(8,128)(2,1)}), bf16[4,256,1024]{1,2,0:T(8,128)(2,1)}, u32[]{:S(2)}, u32[]{:S(2)}) async-start(bf16[4,256,1024]{1,2,0:T(8,128)(2,1)} %copy.81), calls=%async_computation.7 | async-start | bytes 4194304 | tf_op jit(solution)/shard_map/all_to_all | solution.py:112
  439.9 8.9 %copy-start.2 = (f32[1024,8,128]{0,2,1:T(8,128)S(1)}, f32[1024,8,128]{0,2,1:T(8,128)}, u32[]{:S(2)}) copy-start(f32[1024,8,128]{0,2,1:T(8,128)} %copy.95) | copy-start | bytes 12582916
  477.1 51.3 %all-to-all-start.6 = ((bf16[4,256,1024]{1,2,0:T(8,128)(2,1)}), bf16[4,256,1024]{1,2,0:T(8,128)(2,1)S(1)}, u32[]{:S(2)}, u32[]{:S(2)}) async-start(bf16[4,256,1024]{1,2,0:T(8,128)(2,1)} %copy.78), calls=%async_computation.6 | async-start | bytes 4194304 | tf_op jit(solution)/shard_map/all_to_all | solution.py:111
Sparse Core Ops, SparseCore 0:
  140.9 36.9 all-gather.4
  326.9 28.1 all-gather.6
where the time goes:
time: 546 us; the launch traced here: 538 us
  waiting for transfers between devices  266 us (49%)
  local copies, waits for them, and re-layouts  110 us (20%)
  matrix products  88 us (16%)
  starting transfers between devices  34.8 us (6%)
  other arithmetic  24.2 us (4%)
  between operations  14.4 us (3%)
    all_to_all x1, waiting for transfers between devices, local(): lax.all_to_all(values, 'head', split_axis=1, concat_axis=0, tiled=True)  44.6 us
    all_to_all x1, waiting for transfers between devices, local(): lax.all_to_all(keys, 'head', split_axis=1, concat_axis=0, tiled=True)  44.1 us
    unnamed x22, local copies, waits for them, and re-layouts  40.2 us
    all_to_all x1, waiting for transfers between devices, local(): lax.all_to_all(grad_q, 'head', split_axis=0, concat_axis=1, tiled=True)  37.6 us
    all_to_all x1, waiting for transfers between devices, local(): lax.all_to_all(grad_out, 'head', split_axis=1, concat_axis=0, tiled=True)  36.2 us
    all_to_all x1, waiting for transfers between devices, local(): lax.all_to_all(grad_k, 'head', split_axis=0, concat_axis=1, tiled=True)  35.5 us
    all_to_all x1, waiting for transfers between devices, local(): lax.all_to_all(queries, 'head', split_axis=1, concat_axis=0, tiled=True)  23.4 us
    all_to_all x1, waiting for transfers between devices, local(): lax.all_to_all(output_head, 'head', split_axis=0, concat_axis=1, tiled=True)  23.4 us
  transfers between devices with their start and end apart: 10, of which 8 were waited for; matrix products, arithmetic and copies ran while one was open for 28% of the time, Pallas kernels for 0%

commit v1 on v0

v1 whole, which is shorter than its diff:
```python
import functools

import jax
import jax.numpy as jnp
from jax import lax
from jax.experimental import pallas as pl
from jax.experimental.pallas import tpu as pltpu
from jax.sharding import PartitionSpec as P

DH = 128
EPSILON = 1e-06
AXES = ("seq", "head")
F32 = jnp.float32
BF16 = jnp.bfloat16


def feature(x):
    xf = x.astype(F32)
    return jnp.where(xf > 0, xf + 1.0, jnp.exp(jnp.minimum(xf, 0.0)))


def slope(x):
    xf = x.astype(F32)
    return jnp.where(xf > 0, 1.0, jnp.exp(jnp.minimum(xf, 0.0)))


def dot(a, b, ca, cb):
    return lax.dot_general(a, b, (((ca,), (cb,)), ((), ())), preferred_element_type=F32)


def causal_mask(rows):
    t = lax.broadcasted_iota(jnp.int32, (rows, rows), 0)
    s = lax.broadcasted_iota(jnp.int32, (rows, rows), 1)
    return t >= s


def cols(j):
    return pl.ds(j * DH, DH)


def own_kernel(hb, k_ref, v_ref, s_ref):
    for j in range(hb):
        k = feature(k_ref[:, cols(j)]).astype(BF16)
        s_ref[cols(j), :] = dot(k, v_ref[:, cols(j)], 0, 0).astype(BF16)


def pre_kernel(hb, q_ref, k_ref, v_ref, ml_ref):
    mask = causal_mask(q_ref.shape[0])
    for j in range(hb):
        q = feature(q_ref[:, cols(j)]).astype(BF16)
        k = feature(k_ref[:, cols(j)]).astype(BF16)
        a = jnp.where(mask, dot(q, k, 1, 1), 0.0).astype(BF16)
        ml_ref[:, cols(j)] = dot(a, v_ref[:, cols(j)], 1, 0)


def fwd_kernel(hb, q_ref, g_ref, ml_ref, p_ref, out_ref, gy_ref, qg_ref):
    for j in range(hb):
        q = feature(q_ref[:, cols(j)]).astype(BF16)
        mixed = ml_ref[:, cols(j)] + dot(q, p_ref[cols(j), :], 1, 0)
        inv = lax.rsqrt(jnp.mean(mixed * mixed, -1, keepdims=True) + EPSILON)
        normed = mixed * inv
        g = g_ref[:, cols(j)].astype(F32)
        gy = inv * (g - normed * jnp.mean(g * normed, -1, keepdims=True))
        gy = gy.astype(BF16)
        out_ref[:, cols(j)] = normed.astype(BF16)
        gy_ref[:, cols(j)] = gy
        qg_ref[cols(j), :] = dot(q, gy, 0, 0).astype(BF16)


def mid_kernel(hb, q_ref, k_ref, v_ref, gy_ref, p_ref, dq_ref, dk_ref, dv_ref):
    mask = causal_mask(q_ref.shape[0])
    for j in range(hb):
        q_raw = q_ref[:, cols(j)]
        q = feature(q_raw).astype(BF16)
        k = feature(k_ref[:, cols(j)]).astype(BF16)
        gy = gy_ref[:, cols(j)]
        m = jnp.where(mask, dot(gy, v_ref[:, cols(j)], 1, 1), 0.0).astype(BF16)
        a = jnp.where(mask, dot(q, k, 1, 1), 0.0).astype(BF16)
        dq = dot(gy, p_ref[cols(j), :], 1, 1) + dot(m, k, 1, 0)
        dq_ref[:, cols(j)] = (dq * slope(q_raw)).astype(BF16)
        dk_ref[:, cols(j)] = dot(m, q, 0, 0)
        dv_ref[:, cols(j)] = dot(a, gy, 0, 0)


def last_kernel(hb, k_ref, v_ref, u_ref, dk_ref, dv_ref, gk_ref, gv_ref):
    for j in range(hb):
        k_raw = k_ref[:, cols(j)]
        k = feature(k_raw).astype(BF16)
        u = u_ref[cols(j), :]
        dk = dk_ref[:, cols(j)] + dot(v_ref[:, cols(j)], u, 1, 1)
        gk_ref[:, cols(j)] = (dk * slope(k_raw)).astype(BF16)
        gv_ref[:, cols(j)] = (dv_ref[:, cols(j)] + dot(k, u, 1, 0)).astype(BF16)


def scan_kernel(n, reverse, x_ref, o_ref):
    r = x_ref.shape[0] // n
    total = jnp.zeros((r, DH), F32)
    for i in range(n):
        at = pl.ds((n - 1 - i if reverse else i) * r, r)
        o_ref[at, :] = total.astype(BF16)
        total = total + x_ref[at, :].astype(F32)


def exclusive_scan(state, n, reverse):
    rows = state.shape[0]
    x = lax.all_to_all(state, AXES, 0, 0, tiled=True)
    vm = pl.BlockSpec(memory_space=pltpu.VMEM)
    y = pl.pallas_call(
        functools.partial(scan_kernel, n, reverse),
        out_shape=jax.ShapeDtypeStruct((rows, DH), BF16),
        in_specs=[vm],
        out_specs=vm,
        name="scan",
    )(x)
    return lax.all_to_all(y, AXES, 0, 0, tiled=True)


def local(queries, keys, values, grad_out):
    n = lax.axis_size("seq") * lax.axis_size("head")
    rows, width = queries.shape
    heads = width // DH
    hb = 4
    tok = pl.BlockSpec((rows, hb * DH), lambda i: (0, i))
    st = pl.BlockSpec((hb * DH, DH), lambda i: (i, 0))
    wide = lambda dt: jax.ShapeDtypeStruct((rows, width), dt)
    state = jax.ShapeDtypeStruct((width, DH), BF16)

    def call(kernel, ins, outs, shapes, name, flops, nbytes):
        return pl.pallas_call(
            functools.partial(kernel, hb),
            grid=(heads // hb,),
            in_specs=ins,
            out_specs=outs,
            out_shape=shapes,
            name=name,
            cost_estimate=pl.CostEstimate(
                flops=flops * heads * rows * DH, bytes_accessed=nbytes * rows * width, transcendentals=0
            ),
        )

    own = call(own_kernel, [tok, tok], st, state, "own", 2 * DH, 5)(keys, values)
    prefix = exclusive_scan(own, n, False)
    mixed_local = call(pre_kernel, [tok] * 3, tok, wide(F32), "pre", 4 * rows, 10)(queries, keys, values)
    output, gy, qg = call(
        fwd_kernel, [tok, tok, tok, st], [tok, tok, st], [wide(BF16), wide(BF16), state], "fwd", 4 * DH, 14
    )(queries, grad_out, mixed_local, prefix)
    suffix = exclusive_scan(qg, n, True)
    grad_q, dk, dv = call(
        mid_kernel, [tok] * 4 + [st], [tok] * 3, [wide(BF16), wide(F32), wide(F32)], "mid", 10 * rows + 2 * DH, 20
    )(queries, keys, values, gy, prefix)
    grad_k, grad_v = call(
        last_kernel, [tok, tok, st, tok, tok], [tok, tok], [wide(BF16), wide(BF16)], "last", 4 * DH, 17
    )(keys, values, suffix, dk, dv)
    return (output, grad_q, grad_k, grad_v)


def solution(mesh):
    placed = (P(AXES, None),) * 4
    return jax.shard_map(local, mesh=mesh, in_specs=placed, out_specs=placed, check_vma=False)
```

time: 546 us -> 157 us (0.29)
  the two profiles are of different devices: /device:TPU:6 before, /device:TPU:1 now
where the time goes in v1:
time: 157 us; the launch traced here: 156 us
  blocking collectives  63.1 us (40%)
  Pallas kernels  54.6 us (35%)
  waiting for transfers between devices  29 us (18%)
  starting transfers between devices  6.3 us (4%)
  local copies, waits for them, and re-layouts  2.03 us (1%)
    all_to_all x2, blocking collectives, exclusive_scan(): x = lax.all_to_all(state, AXES, 0, 0, tiled=True)  63.1 us
    all_to_all x2, waiting for transfers between devices, exclusive_scan(): return lax.all_to_all(y, AXES, 0, 0, tiled=True)  29 us
    pallas_call x1, Pallas kernels, local(): call(mid_kernel, [tok] * 4 + [st], [tok] * 3, [wide(BF16), wide(F32), wid...  14.2 us
    pallas_call x1, Pallas kernels, local(): call(fwd_kernel, [tok, tok, tok, st], [tok, tok, st], [wide(BF16), wide(B...  9.65 us
    pallas_call x1, Pallas kernels, local(): call(pre_kernel, [tok] * 3, tok, wide(F32), 'pre', 4 * rows, 10)  9.48 us
    pallas_call x1, Pallas kernels, local(): call(last_kernel, [tok, tok, st, tok, tok], [tok, tok], [wide(BF16), wide...  9.47 us
    pallas_call x1, Pallas kernels, local(): call(own_kernel, [tok, tok], st, state, 'own', 2 * DH, 5)(keys, values)  7.04 us
    all_to_all x2, starting transfers between devices, exclusive_scan(): return lax.all_to_all(y, AXES, 0, 0, tiled=True)  6.3 us
  transfers between devices with their start and end apart: 2, of which 2 were waited for; matrix products, arithmetic and copies ran while one was open for 0% of the time, Pallas kernels for 15%

profile of v1, /device:TPU:1, one launch (start us, length us, event | category | flops | bytes accessed | tf_op | source)
XLA Modules:
  0.0 155.7 jit_solution(6758555988534482341)
XLA Ops:
  0.6 7.0 %own.1 = bf16[4096,128]{1,0:T(8,128)(2,1)} custom-call(bf16[256,4096]{1,0:T(8,128)(2,1)} %k_ref.7, bf16[256,4096]{1,0:T(8,128)(2,1)} %v_ref.7), custom_call_target="tpu_custom_call" | custom-call | flops 268435456 | bytes 5242880 | tf_op jit(solution)/shard_map/own/pallas_call | solution.py:141
  7.7 33.5 %all_to_all.44 = bf16[32,128,128]{2,1,0:T(8,128)(2,1)} all-to-all(bf16[32,128,128]{2,1,0:T(8,128)(2,1)} %bitcast.10), channel_id=1, replica_groups=mesh['seq'=8,'head'=4] {'seq','head'}, dimensions={0} | all-to-all | bytes 2097152 | tf_op jit(solution)/shard_map/all_to_all | solution.py:106
  41.2 2.4 %scan.2 = bf16[4096,128]{1,0:T(8,128)(2,1)} custom-call(bf16[4096,128]{1,0:T(8,128)(2,1)} %bitcast.13), custom_call_target="tpu_custom_call" | custom-call | tf_op jit(solution)/shard_map/scan/pallas_call | solution.py:108
  43.6 3.2 %all-to-all-start.1 = ((bf16[32,128,128]{2,1,0:T(8,128)(2,1)}), bf16[32,128,128]{2,1,0:T(8,128)(2,1)S(1)}, u32[]{:S(2)}, u32[]{:S(2)}) async-start(bf16[32,128,128]{2,1,0:T(8,128)(2,1)} %bitcast.12), calls=%async_computation.1 | async-start | bytes 2097152 | tf_op jit(solution)/shard_map/all_to_all | solution.py:115
  46.7 9.5 %pre.1.ml_ref = f32[256,4096]{1,0:T(8,128)} custom-call(bf16[256,4096]{1,0:T(8,128)(2,1)} %q_ref.5, bf16[256,4096]{1,0:T(8,128)(2,1)} %k_ref.7, bf16[256,4096]{1,0:T(8,128)(2,1)} %v_ref.7), custom_call_target="tpu_custom_call" | custom-call | flops 1073741824 | bytes 10485760 | tf_op jit(solution)/shard_map/pre/pallas_call | solution.py:143
  56.2 16.9 %all-to-all-done.1 = bf16[32,128,128]{2,1,0:T(8,128)(2,1)S(1)} async-done(((bf16[32,128,128]{2,1,0:T(8,128)(2,1)}), bf16[32,128,128]{2,1,0:T(8,128)(2,1)S(1)}, u32[]{:S(2)}, u32[]{:S(2)}) %all-to-all-start.1) | async-done | bytes 1048608 | tf_op jit(solution)/shard_map/all_to_all | solution.py:115
  73.0 0.0 copy-start
  73.0 1.0 copy-done
  74.0 9.7 %fwd.1 = (bf16[256,4096]{1,0:T(8,128)(2,1)}, bf16[256,4096]{1,0:T(8,128)(2,1)}, bf16[4096,128]{1,0:T(8,128)(2,1)}) custom-call(bf16[256,4096]{1,0:T(8,128)(2,1)} %q_ref.5, bf16[256,4096]{1,0:T(8,128)(2,1)} %g_ref.1, f32[256,4096]{1,0:T(8,128)} %pre.1.ml_ref, bf16[4096,128]{1,0:T(8,128)(2,1)} %bitcast.8), custom_call_target="tpu_custom_call" | custom-call | flops 536870912 | bytes 14680064 | tf_op jit(solution)/shard_map/fwd/pallas_call | solution.py:144
  83.7 29.6 %all_to_all.45 = bf16[32,128,128]{2,1,0:T(8,128)(2,1)} all-to-all(bf16[32,128,128]{2,1,0:T(8,128)(2,1)} %bitcast.16), channel_id=1, replica_groups=mesh['seq'=8,'head'=4] {'seq','head'}, dimensions={0} | all-to-all | bytes 2097152 | tf_op jit(solution)/shard_map/all_to_all | solution.py:106
  113.3 2.5 %scan.3 = bf16[4096,128]{1,0:T(8,128)(2,1)} custom-call(bf16[4096,128]{1,0:T(8,128)(2,1)} %bitcast.14), custom_call_target="tpu_custom_call" | custom-call | tf_op jit(solution)/shard_map/scan/pallas_call | solution.py:108
  115.7 3.2 %all-to-all-start.3 = ((bf16[32,128,128]{2,1,0:T(8,128)(2,1)}), bf16[32,128,128]{2,1,0:T(8,128)(2,1)S(1)}, u32[]{:S(2)}, u32[]{:S(2)}) async-start(bf16[32,128,128]{2,1,0:T(8,128)(2,1)} %bitcast.11), calls=%async_computation.3 | async-start | bytes 2097152 | tf_op jit(solution)/shard_map/all_to_all | solution.py:115
  118.9 14.2 %mid.1 = (bf16[256,4096]{1,0:T(8,128)(2,1)}, f32[256,4096]{1,0:T(8,128)}, f32[256,4096]{1,0:T(8,128)}) custom-call(bf16[256,4096]{1,0:T(8,128)(2,1)} %q_ref.5, bf16[256,4096]{1,0:T(8,128)(2,1)} %k_ref.7, bf16[256,4096]{1,0:T(8,128)(2,1)} %v_ref.7, bf16[256,4096]{1,0:T(8,128)(2,1)} %get-tuple-element.13.gy_ref, bf16[4096,128]{1,0:T(8,128)(2,1)} %bitcast.9), custom_call_target="tpu_custom_call" | custom-call | flops 2952790016 | bytes 20971520 | tf_op jit(solution)/shard_map/mid/pallas_call | solution.py:148
  133.0 12.1 %all-to-all-done.3 = bf16[32,128,128]{2,1,0:T(8,128)(2,1)S(1)} async-done(((bf16[32,128,128]{2,1,0:T(8,128)(2,1)}), bf16[32,128,128]{2,1,0:T(8,128)(2,1)S(1)}, u32[]{:S(2)}, u32[]{:S(2)}) %all-to-all-start.3) | async-done | bytes 1048608 | tf_op jit(solution)/shard_map/all_to_all | solution.py:115
  145.2 0.0 copy-start.1
  145.2 1.1 copy-done.1
  146.3 9.5 %last.1 = (bf16[256,4096]{1,0:T(8,128)(2,1)}, bf16[256,4096]{1,0:T(8,128)(2,1)}) custom-call(bf16[256,4096]{1,0:T(8,128)(2,1)} %k_ref.7, bf16[256,4096]{1,0:T(8,128)(2,1)} %v_ref.7, bf16[4096,128]{1,0:T(8,128)(2,1)} %bitcast.15, f32[256,4096]{1,0:T(8,128)} %get-tuple-element.16.dk_ref, f32[256,4096]{1,0:T(8,128)} %get-tuple-element.17.dv_ref), custom_call_target="tpu_custom_call" | custom-call | flops 536870912 | bytes 17825792 | tf_op jit(solution)/shard_map/last/pallas_call | solution.py:151
Async XLA Ops:
  43.6 29.5 %all-to-all-start.1 = ((bf16[32,128,128]{2,1,0:T(8,128)(2,1)}), bf16[32,128,128]{2,1,0:T(8,128)(2,1)S(1)}, u32[]{:S(2)}, u32[]{:S(2)}) async-start(bf16[32,128,128]{2,1,0:T(8,128)(2,1)} %bitcast.12), calls=%async_computation.1 | async-start | bytes 2097152 | tf_op jit(solution)/shard_map/all_to_all | solution.py:115
  73.0 1.0 copy-start
  115.7 29.5 %all-to-all-start.3 = ((bf16[32,128,128]{2,1,0:T(8,128)(2,1)}), bf16[32,128,128]{2,1,0:T(8,128)(2,1)S(1)}, u32[]{:S(2)}, u32[]{:S(2)}) async-start(bf16[32,128,128]{2,1,0:T(8,128)(2,1)} %bitcast.11), calls=%async_computation.3 | async-start | bytes 2097152 | tf_op jit(solution)/shard_map/all_to_all | solution.py:115
  145.2 1.1 copy-start.1

commit v2 on v1

v2 whole, which is shorter than its diff:
```python
import functools

import jax
import jax.numpy as jnp
from jax import lax
from jax.experimental import pallas as pl
from jax.experimental.pallas import tpu as pltpu
from jax.sharding import PartitionSpec as P

DH = 128
EPSILON = 1e-06
AXES = ("seq", "head")
F32 = jnp.float32
BF16 = jnp.bfloat16
STEP = 8
VMEM_LIMIT = 24 * 1024 * 1024


def feature(x):
    return jnp.where(x > 0, x + jnp.ones((), BF16), jnp.exp(x.astype(F32)).astype(BF16))


def feature_slope(x):
    xf = x.astype(F32)
    up = xf > 0
    e = jnp.exp(jnp.minimum(xf, 0.0))
    return jnp.where(up, xf + 1.0, e).astype(BF16), jnp.where(up, 1.0, e)


def dot(a, b, ca, cb):
    return lax.dot_general(a, b, (((ca,), (cb,)), ((), ())), preferred_element_type=F32)


def causal_mask(rows):
    t = lax.broadcasted_iota(jnp.int32, (rows, rows), 0)
    s = lax.broadcasted_iota(jnp.int32, (rows, rows), 1)
    return t >= s


def own_body(k, v):
    return (dot(feature(k), v, 0, 0).astype(BF16),)


def pre_body(q, k, v):
    qf = feature(q)
    kf = feature(k)
    a = jnp.where(causal_mask(q.shape[0]), dot(qf, kf, 1, 1), 0.0).astype(BF16)
    return (dot(a, v, 1, 0).astype(BF16),)


def fwd_body(q, g, mixed_local, p):
    qf = feature(q)
    mixed = mixed_local.astype(F32) + dot(qf, p, 1, 0)
    gf = g.astype(F32)
    inv = lax.rsqrt(jnp.mean(mixed * mixed, -1, keepdims=True) + EPSILON)
    normed = mixed * inv
    gy = (inv * (gf - normed * jnp.mean(gf * normed, -1, keepdims=True))).astype(BF16)
    return normed.astype(BF16), gy, dot(qf, gy, 0, 0).astype(BF16)


def mid_body(q, k, v, gy, p):
    qf, q_slope = feature_slope(q)
    kf = feature(k)
    mask = causal_mask(q.shape[0])
    m = jnp.where(mask, dot(gy, v, 1, 1), 0.0).astype(BF16)
    a = jnp.where(mask, dot(qf, kf, 1, 1), 0.0).astype(BF16)
    dq = dot(gy, p, 1, 1) + dot(m, kf, 1, 0)
    return (dq * q_slope).astype(BF16), dot(m, qf, 0, 0).astype(BF16), dot(a, gy, 0, 0).astype(BF16)


def last_body(k, v, u, dk, dv):
    kf, k_slope = feature_slope(k)
    dk = dk.astype(F32) + dot(v, u, 1, 1)
    dv = dv.astype(F32) + dot(kf, u, 1, 0)
    return (dk * k_slope).astype(BF16), dv.astype(BF16)


def chunk(ref, at, size, tall):
    piece = pl.ds(pl.multiple_of(at * size, size), size)
    return ref.at[piece, :] if tall else ref.at[:, piece]


def stream_kernel(body, step, tall_in, tall_out, held_in, held_out, *refs):
    refs = list(refs)
    take = lambda count: [refs.pop(0) for _ in range(count)]
    ni, no = len(tall_in), len(tall_out)
    ins, outs = take(ni), take(no)
    in_bufs = [r if held else refs.pop(0) for r, held in zip(ins, held_in)]
    out_bufs = [r if held else refs.pop(0) for r, held in zip(outs, held_out)]
    in_sem, out_sem = refs
    moved_in = [i for i in range(ni) if not held_in[i]]
    moved_out = [i for i in range(no) if not held_out[i]]
    size = step * DH
    steps = in_bufs[0].shape[0 if tall_in[0] else 1] // size

    def fetch(i, c):
        return pltpu.make_async_copy(
            chunk(ins[i], c, size, tall_in[i]), chunk(in_bufs[i], c, size, tall_in[i]), in_sem.at[i, c]
        )

    def put(i, c):
        return pltpu.make_async_copy(
            chunk(out_bufs[i], c, size, tall_out[i]), chunk(outs[i], c, size, tall_out[i]), out_sem.at[i, c]
        )

    @pl.loop(0, steps)
    def _(c):
        for i in moved_in:
            fetch(i, c).start()

    @pl.loop(0, steps)
    def _(c):
        for i in moved_in:
            fetch(i, c).wait()
        for j in range(step):
            at = c * step + j
            values = [chunk(in_bufs[i], at, DH, tall_in[i])[...] for i in range(ni)]
            for i, value in enumerate(body(*values)):
                chunk(out_bufs[i], at, DH, tall_out[i])[...] = value
        for i in moved_out:
            put(i, c).start()

    @pl.loop(0, steps)
    def _(c):
        for i in moved_out:
            put(i, c).wait()


def stream(body, name, args, outs, step, flops, held_in=(), held_out=()):
    width = args[0].shape[1]
    held_in = [i in held_in for i in range(len(args))]
    held_out = [i in held_out for i in range(len(outs))]
    tall_in = [a.shape[1] == DH for a in args]
    tall_out = [o.shape[1] == DH for o in outs]
    steps = width // DH // step
    nbytes = sum(a.size * a.dtype.itemsize for a in args) + sum(o.size * o.dtype.itemsize for o in outs)
    spec = lambda held: pl.BlockSpec(memory_space=pltpu.VMEM if held else pltpu.HBM)
    place = lambda a, held: pltpu.with_memory_space_constraint(a, pltpu.VMEM if held else pltpu.HBM)
    bufs = [pltpu.VMEM(a.shape, a.dtype) for a, h in zip(args, held_in) if not h]
    bufs += [pltpu.VMEM(o.shape, o.dtype) for o, h in zip(outs, held_out) if not h]
    return pl.pallas_call(
        functools.partial(stream_kernel, body, step, tall_in, tall_out, held_in, held_out),
        in_specs=[spec(h) for h in held_in],
        out_specs=[spec(h) for h in held_out],
        out_shape=[(pltpu.VMEM if h else pltpu.HBM)(o.shape, o.dtype) for o, h in zip(outs, held_out)],
        scratch_shapes=bufs
        + [pltpu.SemaphoreType.DMA((len(args), steps)), pltpu.SemaphoreType.DMA((len(outs), steps))],
        name=name,
        compiler_params=pltpu.CompilerParams(vmem_limit_bytes=VMEM_LIMIT),
        cost_estimate=pl.CostEstimate(
            flops=flops * width * args[0].shape[0], bytes_accessed=nbytes, transcendentals=0
        ),
    )(*[place(a, h) for a, h in zip(args, held_in)])


def scan_kernel(n, reverse, x_ref, o_ref, buf, sem):
    r = x_ref.shape[0] // n
    parts = 4 if n % 4 == 0 else 1
    span = n // parts
    total = jnp.zeros((r, DH), F32)
    copies = []
    for part in range(parts):
        for i in range(part * span, (part + 1) * span):
            at = pl.ds((n - 1 - i if reverse else i) * r, r)
            buf[at, :] = total.astype(BF16)
            total = total + x_ref[at, :].astype(F32)
        at = pl.ds((parts - 1 - part if reverse else part) * span * r, span * r)
        copies.append(pltpu.make_async_copy(buf.at[at, :], o_ref.at[at, :], sem.at[part]))
        copies[-1].start()
    for copy in copies:
        copy.wait()


def exclusive_scan(state, n, reverse):
    rows = state.shape[0]
    x = lax.all_to_all(state, AXES, 0, 0, tiled=True)
    y = pl.pallas_call(
        functools.partial(scan_kernel, n, reverse),
        out_shape=pltpu.HBM((rows, DH), BF16),
        in_specs=[pl.BlockSpec(memory_space=pltpu.VMEM)],
        out_specs=pl.BlockSpec(memory_space=pltpu.HBM),
        scratch_shapes=[pltpu.VMEM((rows, DH), BF16), pltpu.SemaphoreType.DMA((4,))],
        name="scan",
        compiler_params=pltpu.CompilerParams(vmem_limit_bytes=VMEM_LIMIT),
    )(pltpu.with_memory_space_constraint(x, pltpu.VMEM))
    return lax.all_to_all(y, AXES, 0, 0, tiled=True)


def local(queries, keys, values, grad_out):
    n = lax.axis_size("seq") * lax.axis_size("head")
    rows, width = queries.shape
    wide = lambda dt: jax.ShapeDtypeStruct((rows, width), dt)
    state = jax.ShapeDtypeStruct((width, DH), BF16)

    (own,) = stream(own_body, "own", [keys, values], [state], STEP, 2 * DH)
    prefix = exclusive_scan(own, n, False)
    (mixed_local,) = stream(pre_body, "pre", [queries, keys, values], [wide(BF16)], STEP, 4 * rows)
    output, gy, qg = stream(
        fwd_body,
        "fwd",
        [queries, grad_out, mixed_local, prefix],
        [wide(BF16), wide(BF16), state],
        STEP,
        4 * DH,
        (3,),
    )
    suffix = exclusive_scan(qg, n, True)
    grad_q, dk, dv = stream(
        mid_body, "mid", [queries, keys, values, gy, prefix], [wide(BF16), wide(BF16), wide(BF16)], STEP, 10 * rows
    )
    grad_k, grad_v = stream(
        last_body, "last", [keys, values, suffix, dk, dv], [wide(BF16), wide(BF16)], STEP, 4 * DH, (2,)
    )
    return (output, grad_q, grad_k, grad_v)


def solution(mesh):
    placed = (P(AXES, None),) * 4
    return jax.shard_map(local, mesh=mesh, in_specs=placed, out_specs=placed, check_vma=False)
```

time: 157 us -> 144 us (0.917)
  Pallas kernels: 54.6 us -> 40.1 us
  waiting for transfers between devices: 29 us -> 33 us
  local copies, waits for them, and re-layouts: 2.03 us -> 0.01 us
    pallas_call x7, Pallas kernels: 54.6 us -> 40.1 us  [the longest x5 38 us: stream(): pl.pallas_call(functools.partial(stream_kernel, body, step, tall_in, tall...]
    all_to_all x2, waiting for transfers between devices: 29 us -> 33 us  [exclusive_scan(): return lax.all_to_all(y, AXES, 0, 0, tiled=True)]
    unnamed x4 -> x2, local copies, waits for them, and re-layouts: 2.03 us -> 0.01 us
  transfers between devices with their start and end apart: 2 -> 2, of which waited for: 2 -> 2; matrix products, arithmetic and copies ran while one was open for 0% -> 0% of each run, Pallas kernels for 15% -> 14%
where the time goes in v2:
time: 144 us; the launch traced here: 143 us
  blocking collectives  62.9 us (44%)
  Pallas kernels  40.1 us (28%)
  waiting for transfers between devices  33 us (23%)
  starting transfers between devices  6.31 us (4%)
    all_to_all x2, blocking collectives, exclusive_scan(): x = lax.all_to_all(state, AXES, 0, 0, tiled=True)  62.9 us
    pallas_call x5, Pallas kernels, stream(): pl.pallas_call(functools.partial(stream_kernel, body, step, tall_in, tall...  38 us
    all_to_all x2, waiting for transfers between devices, exclusive_scan(): return lax.all_to_all(y, AXES, 0, 0, tiled=True)  33 us
    all_to_all x2, starting transfers between devices, exclusive_scan(): return lax.all_to_all(y, AXES, 0, 0, tiled=True)  6.31 us
  transfers between devices with their start and end apart: 2, of which 2 were waited for; matrix products, arithmetic and copies ran while one was open for 0% of the time, Pallas kernels for 14%

profile of v2, /device:TPU:1, one launch (start us, length us, event | category | flops | bytes accessed | tf_op | source)
XLA Modules:
  0.0 143.1 jit_solution(2679190126000054416)
XLA Ops:
  0.6 4.0 %own.1 = bf16[4096,128]{1,0:T(8,128)(2,1)} custom-call(bf16[256,4096]{1,0:T(8,128)(2,1)} %refs_0_.9, bf16[256,4096]{1,0:T(8,128)(2,1)} %refs_1_.9), custom_call_target="tpu_custom_call" | custom-call | flops 268435456 | bytes 5242880 | tf_op jit(solution)/shard_map/own/pallas_call | solution.py:141
  4.7 33.4 %all_to_all.44 = bf16[32,128,128]{2,1,0:T(8,128)(2,1)S(1)} all-to-all(bf16[32,128,128]{2,1,0:T(8,128)(2,1)} %bitcast.13), channel_id=1, replica_groups=mesh['seq'=8,'head'=4] {'seq','head'}, dimensions={0} | all-to-all | bytes 2097152 | tf_op jit(solution)/shard_map/all_to_all | solution.py:176
  38.1 1.0 scan.2
  39.1 3.2 %all-to-all-start.1 = ((bf16[32,128,128]{2,1,0:T(8,128)(2,1)}), bf16[32,128,128]{2,1,0:T(8,128)(2,1)S(1)}, u32[]{:S(2)}, u32[]{:S(2)}) async-start(bf16[32,128,128]{2,1,0:T(8,128)(2,1)} %bitcast.15), calls=%async_computation.1 | async-start | bytes 2097152 | tf_op jit(solution)/shard_map/all_to_all | solution.py:186
  42.3 6.2 %pre.1.refs_2_ = bf16[256,4096]{1,0:T(8,128)(2,1)} custom-call(bf16[256,4096]{1,0:T(8,128)(2,1)} %refs_0_.8, bf16[256,4096]{1,0:T(8,128)(2,1)} %refs_0_.9, bf16[256,4096]{1,0:T(8,128)(2,1)} %refs_1_.9), custom_call_target="tpu_custom_call" | custom-call | flops 1073741824 | bytes 8388608 | tf_op jit(solution)/shard_map/pre/pallas_call | solution.py:141
  48.5 20.1 %all-to-all-done.1 = bf16[32,128,128]{2,1,0:T(8,128)(2,1)S(1)} async-done(((bf16[32,128,128]{2,1,0:T(8,128)(2,1)}), bf16[32,128,128]{2,1,0:T(8,128)(2,1)S(1)}, u32[]{:S(2)}, u32[]{:S(2)}) %all-to-all-start.1) | async-done | bytes 1048608 | tf_op jit(solution)/shard_map/all_to_all | solution.py:186
  68.6 0.0 copy-start
  68.6 8.5 %fwd.1 = (bf16[256,4096]{1,0:T(8,128)(2,1)}, bf16[256,4096]{1,0:T(8,128)(2,1)}, bf16[4096,128]{1,0:T(8,128)(2,1)}) custom-call(bf16[256,4096]{1,0:T(8,128)(2,1)} %refs_0_.8, bf16[256,4096]{1,0:T(8,128)(2,1)} %refs_1_.7, bf16[256,4096]{1,0:T(8,128)(2,1)} %pre.1.refs_2_, bf16[4096,128]{1,0:T(8,128)(2,1)S(1)} %bitcast.8), custom_call_target="tpu_custom_call" | custom-call | flops 536870912 | bytes 12582912 | tf_op jit(solution)/shard_map/fwd/pallas_call | solution.py:141
  77.1 0.0 copy-done
  77.1 29.5 %all_to_all.45 = bf16[32,128,128]{2,1,0:T(8,128)(2,1)S(1)} all-to-all(bf16[32,128,128]{2,1,0:T(8,128)(2,1)} %bitcast.16), channel_id=1, replica_groups=mesh['seq'=8,'head'=4] {'seq','head'}, dimensions={0} | all-to-all | bytes 2097152 | tf_op jit(solution)/shard_map/all_to_all | solution.py:176
  106.6 1.0 scan.3
  107.7 3.2 %all-to-all-start.3 = ((bf16[32,128,128]{2,1,0:T(8,128)(2,1)}), bf16[32,128,128]{2,1,0:T(8,128)(2,1)S(1)}, u32[]{:S(2)}, u32[]{:S(2)}) async-start(bf16[32,128,128]{2,1,0:T(8,128)(2,1)} %bitcast.14), calls=%async_computation.3 | async-start | bytes 2097152 | tf_op jit(solution)/shard_map/all_to_all | solution.py:186
  110.8 13.5 %mid.1 = (bf16[256,4096]{1,0:T(8,128)(2,1)}, bf16[256,4096]{1,0:T(8,128)(2,1)}, bf16[256,4096]{1,0:T(8,128)(2,1)}) custom-call(bf16[256,4096]{1,0:T(8,128)(2,1)} %refs_0_.8, bf16[256,4096]{1,0:T(8,128)(2,1)} %refs_0_.9, bf16[256,4096]{1,0:T(8,128)(2,1)} %refs_1_.9, bf16[256,4096]{1,0:T(8,128)(2,1)} %get-tuple-element.13.refs_3_, bf16[4096,128]{1,0:T(8,128)(2,1)} %bitcast.9), custom_call_target="tpu_custom_call" | custom-call | flops 2684354560 | bytes 15728640 | tf_op jit(solution)/shard_map/mid/pallas_call | solution.py:141
  124.3 12.9 %all-to-all-done.3 = bf16[32,128,128]{2,1,0:T(8,128)(2,1)S(1)} async-done(((bf16[32,128,128]{2,1,0:T(8,128)(2,1)}), bf16[32,128,128]{2,1,0:T(8,128)(2,1)S(1)}, u32[]{:S(2)}, u32[]{:S(2)}) %all-to-all-start.3) | async-done | bytes 1048608 | tf_op jit(solution)/shard_map/all_to_all | solution.py:186
  137.1 5.9 %last.1 = (bf16[256,4096]{1,0:T(8,128)(2,1)}, bf16[256,4096]{1,0:T(8,128)(2,1)}) custom-call(bf16[256,4096]{1,0:T(8,128)(2,1)} %refs_0_.9, bf16[256,4096]{1,0:T(8,128)(2,1)} %refs_1_.9, bf16[4096,128]{1,0:T(8,128)(2,1)S(1)} %bitcast.10, bf16[256,4096]{1,0:T(8,128)(2,1)} %get-tuple-element.16.refs_3_, bf16[256,4096]{1,0:T(8,128)(2,1)} %get-tuple-element.17.refs_4_), custom_call_target="tpu_custom_call" | custom-call | flops 536870912 | bytes 13631488 | tf_op jit(solution)/shard_map/last/pallas_call | solution.py:141
Async XLA Ops:
  39.1 29.5 %all-to-all-start.1 = ((bf16[32,128,128]{2,1,0:T(8,128)(2,1)}), bf16[32,128,128]{2,1,0:T(8,128)(2,1)S(1)}, u32[]{:S(2)}, u32[]{:S(2)}) async-start(bf16[32,128,128]{2,1,0:T(8,128)(2,1)} %bitcast.15), calls=%async_computation.1 | async-start | bytes 2097152 | tf_op jit(solution)/shard_map/all_to_all | solution.py:186
  68.6 8.5 %copy-start = (bf16[32,128,128]{2,1,0:T(8,128)(2,1)}, bf16[32,128,128]{2,1,0:T(8,128)(2,1)S(1)}, u32[]{:S(2)}) copy-start(bf16[32,128,128]{2,1,0:T(8,128)(2,1)S(1)} %all-to-all-done.1) | copy-start | bytes 3145732
  107.7 29.5 %all-to-all-start.3 = ((bf16[32,128,128]{2,1,0:T(8,128)(2,1)}), bf16[32,128,128]{2,1,0:T(8,128)(2,1)S(1)}, u32[]{:S(2)}, u32[]{:S(2)}) async-start(bf16[32,128,128]{2,1,0:T(8,128)(2,1)} %bitcast.14), calls=%async_computation.3 | async-start | bytes 2097152 | tf_op jit(solution)/shard_map/all_to_all | solution.py:186

commit v3 on v2

--- a/solution.py
+++ b/solution.py
@@ -38,40 +38,49 @@
 
 
 def own_body(k, v):
-    return (dot(feature(k), v, 0, 0).astype(BF16),)
-
-
-def pre_body(q, k, v):
+    return (dot(v, feature(k), 0, 0).astype(BF16),)
+
+
+def pre_body(q, k, v, g):
     qf = feature(q)
+    a = jnp.where(causal_mask(q.shape[0]), dot(qf, feature(k), 1, 1), 0.0).astype(BF16)
+    return dot(v, a, 0, 1).astype(BF16), g.T, qf
+
+
+def normalize(qf, g, mixed_local, p):
+    cuts = [slice(i, i + DH) for i in range(0, p.shape[0], DH)]
+    shape = (len(cuts), DH, qf.shape[0])
+    mixed = mixed_local.astype(F32) + jnp.concatenate([dot(p[h], qf[:, h], 1, 1) for h in cuts], 0)
+    mixed = mixed.reshape(shape)
+    gf = g.astype(F32).reshape(shape)
+    inv = lax.rsqrt(jnp.mean(mixed * mixed, 1, keepdims=True) + EPSILON)
+    gy = inv * (gf - mixed * (inv * (inv * jnp.mean(gf * mixed, 1, keepdims=True))))
+    return mixed * inv, gy.astype(BF16)
+
+
+def fwd_body(qf, g, mixed_local, p):
+    _, gy = normalize(qf, g, mixed_local, p)
+    states = [dot(gy[i], qf[:, i * DH : (i + 1) * DH], 1, 0) for i in range(gy.shape[0])]
+    return (jnp.concatenate(states, 0).astype(BF16),)
+
+
+def mid_body(q, k, v, g, mixed_local, p):
+    qf, q_slope = feature_slope(q)
+    normed, gy = normalize(qf, g, mixed_local, p)
     kf = feature(k)
-    a = jnp.where(causal_mask(q.shape[0]), dot(qf, kf, 1, 1), 0.0).astype(BF16)
-    return (dot(a, v, 1, 0).astype(BF16),)
-
-
-def fwd_body(q, g, mixed_local, p):
-    qf = feature(q)
-    mixed = mixed_local.astype(F32) + dot(qf, p, 1, 0)
-    gf = g.astype(F32)
-    inv = lax.rsqrt(jnp.mean(mixed * mixed, -1, keepdims=True) + EPSILON)
-    normed = mixed * inv
-    gy = (inv * (gf - normed * jnp.mean(gf * normed, -1, keepdims=True))).astype(BF16)
-    return normed.astype(BF16), gy, dot(qf, gy, 0, 0).astype(BF16)
-
-
-def mid_body(q, k, v, gy, p):
-    qf, q_slope = feature_slope(q)
-    kf = feature(k)
+    gy = gy[0].T
     mask = causal_mask(q.shape[0])
     m = jnp.where(mask, dot(gy, v, 1, 1), 0.0).astype(BF16)
     a = jnp.where(mask, dot(qf, kf, 1, 1), 0.0).astype(BF16)
-    dq = dot(gy, p, 1, 1) + dot(m, kf, 1, 0)
-    return (dq * q_slope).astype(BF16), dot(m, qf, 0, 0).astype(BF16), dot(a, gy, 0, 0).astype(BF16)
+    dq = dot(gy, p, 1, 0) + dot(m, kf, 1, 0)
+    output = normed[0].astype(BF16).T
+    return output, (dq * q_slope).astype(BF16), dot(m, qf, 0, 0).astype(BF16), dot(a, gy, 0, 0).astype(BF16)
 
 
 def last_body(k, v, u, dk, dv):
     kf, k_slope = feature_slope(k)
-    dk = dk.astype(F32) + dot(v, u, 1, 1)
-    dv = dv.astype(F32) + dot(kf, u, 1, 0)
+    dk = dk.astype(F32) + dot(v, u, 1, 0)
+    dv = dv.astype(F32) + dot(kf, u, 1, 1)
     return (dk * k_slope).astype(BF16), dv.astype(BF16)
 
 
@@ -80,7 +89,7 @@
     return ref.at[piece, :] if tall else ref.at[:, piece]
 
 
-def stream_kernel(body, step, tall_in, tall_out, held_in, held_out, *refs):
+def stream_kernel(body, step, together, tall_in, tall_out, held_in, held_out, *refs):
     refs = list(refs)
     take = lambda count: [refs.pop(0) for _ in range(count)]
     ni, no = len(tall_in), len(tall_out)
@@ -112,11 +121,12 @@
     def _(c):
         for i in moved_in:
             fetch(i, c).wait()
-        for j in range(step):
-            at = c * step + j
-            values = [chunk(in_bufs[i], at, DH, tall_in[i])[...] for i in range(ni)]
+        span = together * DH
+        for j in range(step // together):
+            at = c * (step // together) + j
+            values = [chunk(in_bufs[i], at, span, tall_in[i])[...] for i in range(ni)]
             for i, value in enumerate(body(*values)):
-                chunk(out_bufs[i], at, DH, tall_out[i])[...] = value
+                chunk(out_bufs[i], at, span, tall_out[i])[...] = value
         for i in moved_out:
             put(i, c).start()
 
@@ -126,12 +136,12 @@
             put(i, c).wait()
 
 
-def stream(body, name, args, outs, step, flops, held_in=(), held_out=()):
+def stream(body, name, args, outs, step, flops, held_in=(), held_out=(), together=1):
     width = args[0].shape[1]
     held_in = [i in held_in for i in range(len(args))]
     held_out = [i in held_out for i in range(len(outs))]
-    tall_in = [a.shape[1] == DH for a in args]
-    tall_out = [o.shape[1] == DH for o in outs]
+    tall_in = [a.shape[0] == width for a in args]
+    tall_out = [o.shape[0] == width for o in outs]
     steps = width // DH // step
     nbytes = sum(a.size * a.dtype.itemsize for a in args) + sum(o.size * o.dtype.itemsize for o in outs)
     spec = lambda held: pl.BlockSpec(memory_space=pltpu.VMEM if held else pltpu.HBM)
@@ -139,7 +149,7 @@
     bufs = [pltpu.VMEM(a.shape, a.dtype) for a, h in zip(args, held_in) if not h]
     bufs += [pltpu.VMEM(o.shape, o.dtype) for o, h in zip(outs, held_out) if not h]
     return pl.pallas_call(
-        functools.partial(stream_kernel, body, step, tall_in, tall_out, held_in, held_out),
+        functools.partial(stream_kernel, body, step, together, tall_in, tall_out, held_in, held_out),
         in_specs=[spec(h) for h in held_in],
         out_specs=[spec(h) for h in held_out],
         out_shape=[(pltpu.VMEM if h else pltpu.HBM)(o.shape, o.dtype) for o, h in zip(outs, held_out)],
@@ -192,21 +202,16 @@
     wide = lambda dt: jax.ShapeDtypeStruct((rows, width), dt)
     state = jax.ShapeDtypeStruct((width, DH), BF16)
 
+    turned = jax.ShapeDtypeStruct((width, rows), BF16)
     (own,) = stream(own_body, "own", [keys, values], [state], STEP, 2 * DH)
     prefix = exclusive_scan(own, n, False)
-    (mixed_local,) = stream(pre_body, "pre", [queries, keys, values], [wide(BF16)], STEP, 4 * rows)
-    output, gy, qg = stream(
-        fwd_body,
-        "fwd",
-        [queries, grad_out, mixed_local, prefix],
-        [wide(BF16), wide(BF16), state],
-        STEP,
-        4 * DH,
-        (3,),
+    mixed_local, grad_turned, query_feat = stream(
+        pre_body, "pre", [queries, keys, values, grad_out], [turned, turned, wide(BF16)], STEP, 4 * rows
     )
+    (qg,) = stream(fwd_body, "fwd", [query_feat, grad_turned, mixed_local, prefix], [state], STEP, 4 * DH, (3,), together=STEP)
     suffix = exclusive_scan(qg, n, True)
-    grad_q, dk, dv = stream(
-        mid_body, "mid", [queries, keys, values, gy, prefix], [wide(BF16), wide(BF16), wide(BF16)], STEP, 10 * rows
+    output, grad_q, dk, dv = stream(
+        mid_body, "mid", [queries, keys, values, grad_turned, mixed_local, prefix], [wide(BF16)] * 4, STEP, 10 * rows
     )
     grad_k, grad_v = stream(
         last_body, "last", [keys, values, suffix, dk, dv], [wide(BF16), wide(BF16)], STEP, 4 * DH, (2,)

time: 144 us -> 141 us (0.979)
  waiting for transfers between devices: 33 us -> 24.4 us
  Pallas kernels: 40.1 us -> 45.8 us
    all_to_all x2, waiting for transfers between devices: 33 us -> 24.4 us  [exclusive_scan(): return lax.all_to_all(y, AXES, 0, 0, tiled=True)]
    pallas_call x5, Pallas kernels: 38 us -> 43.6 us  [stream(): pl.pallas_call(functools.partial(stream_kernel, body, step, together, tal...]
  transfers between devices with their start and end apart: 2 -> 2, of which waited for: 2 -> 2; matrix products, arithmetic and copies ran while one was open for 0% -> 0% of each run, Pallas kernels for 14% -> 20%
where the time goes in v3:
time: 141 us; the launch traced here: 140 us
  blocking collectives  62.9 us (45%)
  Pallas kernels  45.8 us (32%)
  waiting for transfers between devices  24.4 us (17%)
  starting transfers between devices  6.31 us (4%)
    all_to_all x2, blocking collectives, exclusive_scan(): x = lax.all_to_all(state, AXES, 0, 0, tiled=True)  62.9 us
    pallas_call x5, Pallas kernels, stream(): pl.pallas_call(functools.partial(stream_kernel, body, step, together, tal...  43.6 us
    all_to_all x2, waiting for transfers between devices, exclusive_scan(): return lax.all_to_all(y, AXES, 0, 0, tiled=True)  24.4 us
    all_to_all x2, starting transfers between devices, exclusive_scan(): return lax.all_to_all(y, AXES, 0, 0, tiled=True)  6.31 us
  transfers between devices with their start and end apart: 2, of which 2 were waited for; matrix products, arithmetic and copies ran while one was open for 0% of the time, Pallas kernels for 20%

profile of v3, /device:TPU:1, one launch (start us, length us, event | category | flops | bytes accessed | tf_op | source)
XLA Modules:
  0.0 140.1 jit_solution(7009007696557978500)
XLA Ops:
  0.6 4.0 %own.1 = bf16[4096,128]{1,0:T(8,128)(2,1)} custom-call(bf16[256,4096]{1,0:T(8,128)(2,1)} %refs_0_.7, bf16[256,4096]{1,0:T(8,128)(2,1)} %refs_1_.7), custom_call_target="tpu_custom_call" | custom-call | flops 268435456 | bytes 5242880 | tf_op jit(solution)/shard_map/own/pallas_call | solution.py:151
  4.6 33.4 %all_to_all.44 = bf16[32,128,128]{2,1,0:T(8,128)(2,1)S(1)} all-to-all(bf16[32,128,128]{2,1,0:T(8,128)(2,1)} %bitcast.13), channel_id=1, replica_groups=mesh['seq'=8,'head'=4] {'seq','head'}, dimensions={0} | all-to-all | bytes 2097152 | tf_op jit(solution)/shard_map/all_to_all | solution.py:186
  38.0 1.0 scan.2
  39.1 3.2 %all-to-all-start.1 = ((bf16[32,128,128]{2,1,0:T(8,128)(2,1)}), bf16[32,128,128]{2,1,0:T(8,128)(2,1)S(1)}, u32[]{:S(2)}, u32[]{:S(2)}) async-start(bf16[32,128,128]{2,1,0:T(8,128)(2,1)} %bitcast.15), calls=%async_computation.1 | async-start | bytes 2097152 | tf_op jit(solution)/shard_map/all_to_all | solution.py:196
  42.3 6.5 %pre.1 = (bf16[4096,256]{1,0:T(8,128)(2,1)}, bf16[4096,256]{1,0:T(8,128)(2,1)}, bf16[256,4096]{1,0:T(8,128)(2,1)}) custom-call(bf16[256,4096]{1,0:T(8,128)(2,1)} %refs_0_.6, bf16[256,4096]{1,0:T(8,128)(2,1)} %refs_0_.7, bf16[256,4096]{1,0:T(8,128)(2,1)} %refs_1_.7, bf16[256,4096]{1,0:T(8,128)(2,1)} %refs_3_.1), custom_call_target="tpu_custom_call" | custom-call | flops 1073741824 | bytes 14680064 | tf_op jit(solution)/shard_map/pre/pallas_call | solution.py:151
  48.8 19.8 %all-to-all-done.1 = bf16[32,128,128]{2,1,0:T(8,128)(2,1)S(1)} async-done(((bf16[32,128,128]{2,1,0:T(8,128)(2,1)}), bf16[32,128,128]{2,1,0:T(8,128)(2,1)S(1)}, u32[]{:S(2)}, u32[]{:S(2)}) %all-to-all-start.1) | async-done | bytes 1048608 | tf_op jit(solution)/shard_map/all_to_all | solution.py:196
  68.6 0.0 copy-start
  68.6 5.5 %fwd.1 = bf16[4096,128]{1,0:T(8,128)(2,1)} custom-call(bf16[256,4096]{1,0:T(8,128)(2,1)} %get-tuple-element.17.refs_0_, bf16[4096,256]{1,0:T(8,128)(2,1)} %get-tuple-element.13.refs_3_.refs_1_, bf16[4096,256]{1,0:T(8,128)(2,1)} %get-tuple-element.14.refs_4_.refs_2_, bf16[4096,128]{1,0:T(8,128)(2,1)S(1)} %bitcast.8), custom_call_target="tpu_custom_call" | custom-call | flops 536870912 | bytes 8388608 | tf_op jit(solution)/shard_map/fwd/pallas_call | solution.py:151
  74.1 0.0 copy-done
  74.1 29.5 %all_to_all.45 = bf16[32,128,128]{2,1,0:T(8,128)(2,1)S(1)} all-to-all(bf16[32,128,128]{2,1,0:T(8,128)(2,1)} %bitcast.16), channel_id=1, replica_groups=mesh['seq'=8,'head'=4] {'seq','head'}, dimensions={0} | all-to-all | bytes 2097152 | tf_op jit(solution)/shard_map/all_to_all | solution.py:186
  103.7 1.1 scan.3
  104.7 3.2 %all-to-all-start.3 = ((bf16[32,128,128]{2,1,0:T(8,128)(2,1)}), bf16[32,128,128]{2,1,0:T(8,128)(2,1)S(1)}, u32[]{:S(2)}, u32[]{:S(2)}) async-start(bf16[32,128,128]{2,1,0:T(8,128)(2,1)} %bitcast.14), calls=%async_computation.3 | async-start | bytes 2097152 | tf_op jit(solution)/shard_map/all_to_all | solution.py:196
  107.9 21.7 %mid.1 = (bf16[256,4096]{1,0:T(8,128)(2,1)}, bf16[256,4096]{1,0:T(8,128)(2,1)}, bf16[256,4096]{1,0:T(8,128)(2,1)}, bf16[256,4096]{1,0:T(8,128)(2,1)}) custom-call(bf16[256,4096]{1,0:T(8,128)(2,1)} %refs_0_.6, bf16[256,4096]{1,0:T(8,128)(2,1)} %refs_0_.7, bf16[256,4096]{1,0:T(8,128)(2,1)} %refs_1_.7, bf16[4096,256]{1,0:T(8,128)(2,1)} %get-tuple-element.13.refs_3_.refs_1_, ...), custom_call_target="tpu_custom_call" | custom-call | flops 2684354560 | bytes 19922944 | tf_op jit(solution)/shard_map/mid/pallas_call | solution.py:151
  129.6 4.6 %all-to-all-done.3 = bf16[32,128,128]{2,1,0:T(8,128)(2,1)S(1)} async-done(((bf16[32,128,128]{2,1,0:T(8,128)(2,1)}), bf16[32,128,128]{2,1,0:T(8,128)(2,1)S(1)}, u32[]{:S(2)}, u32[]{:S(2)}) %all-to-all-start.3) | async-done | bytes 1048608 | tf_op jit(solution)/shard_map/all_to_all | solution.py:196
  134.2 5.9 %last.1 = (bf16[256,4096]{1,0:T(8,128)(2,1)}, bf16[256,4096]{1,0:T(8,128)(2,1)}) custom-call(bf16[256,4096]{1,0:T(8,128)(2,1)} %refs_0_.7, bf16[256,4096]{1,0:T(8,128)(2,1)} %refs_1_.7, bf16[4096,128]{1,0:T(8,128)(2,1)S(1)} %bitcast.10, bf16[256,4096]{1,0:T(8,128)(2,1)} %get-tuple-element.18.refs_3_, bf16[256,4096]{1,0:T(8,128)(2,1)} %get-tuple-element.19.refs_4_), custom_call_target="tpu_custom_call" | custom-call | flops 536870912 | bytes 13631488 | tf_op jit(solution)/shard_map/last/pallas_call | solution.py:151
Async XLA Ops:
  39.1 29.5 %all-to-all-start.1 = ((bf16[32,128,128]{2,1,0:T(8,128)(2,1)}), bf16[32,128,128]{2,1,0:T(8,128)(2,1)S(1)}, u32[]{:S(2)}, u32[]{:S(2)}) async-start(bf16[32,128,128]{2,1,0:T(8,128)(2,1)} %bitcast.15), calls=%async_computation.1 | async-start | bytes 2097152 | tf_op jit(solution)/shard_map/all_to_all | solution.py:196
  68.6 5.6 %copy-start = (bf16[32,128,128]{2,1,0:T(8,128)(2,1)}, bf16[32,128,128]{2,1,0:T(8,128)(2,1)S(1)}, u32[]{:S(2)}) copy-start(bf16[32,128,128]{2,1,0:T(8,128)(2,1)S(1)} %all-to-all-done.1) | copy-start | bytes 3145732
  104.7 29.5 %all-to-all-start.3 = ((bf16[32,128,128]{2,1,0:T(8,128)(2,1)}), bf16[32,128,128]{2,1,0:T(8,128)(2,1)S(1)}, u32[]{:S(2)}, u32[]{:S(2)}) async-start(bf16[32,128,128]{2,1,0:T(8,128)(2,1)} %bitcast.14), calls=%async_computation.3 | async-start | bytes 2097152 | tf_op jit(solution)/shard_map/all_to_all | solution.py:196

commit v4 on v3

--- a/solution.py
+++ b/solution.py
@@ -38,13 +38,16 @@
 
 
 def own_body(k, v):
-    return (dot(v, feature(k), 0, 0).astype(BF16),)
+    cuts = [slice(i, i + DH) for i in range(0, k.shape[1], DH)]
+    kf = feature(k)
+    return (jnp.concatenate([dot(v[:, h], kf[:, h], 0, 0) for h in cuts], 0).astype(BF16),)
 
 
 def pre_body(q, k, v, g):
     qf = feature(q)
-    a = jnp.where(causal_mask(q.shape[0]), dot(qf, feature(k), 1, 1), 0.0).astype(BF16)
-    return dot(v, a, 0, 1).astype(BF16), g.T, qf
+    kf = feature(k)
+    a = jnp.where(causal_mask(q.shape[0]), dot(qf, kf, 1, 1), 0.0).astype(BF16)
+    return dot(v, a, 0, 1).astype(BF16), g.T, qf, kf
 
 
 def normalize(qf, g, mixed_local, p):
@@ -64,10 +67,9 @@
     return (jnp.concatenate(states, 0).astype(BF16),)
 
 
-def mid_body(q, k, v, g, mixed_local, p):
+def mid_body(q, kf, v, g, mixed_local, p):
     qf, q_slope = feature_slope(q)
     normed, gy = normalize(qf, g, mixed_local, p)
-    kf = feature(k)
     gy = gy[0].T
     mask = causal_mask(q.shape[0])
     m = jnp.where(mask, dot(gy, v, 1, 1), 0.0).astype(BF16)
@@ -77,11 +79,11 @@
     return output, (dq * q_slope).astype(BF16), dot(m, qf, 0, 0).astype(BF16), dot(a, gy, 0, 0).astype(BF16)
 
 
-def last_body(k, v, u, dk, dv):
-    kf, k_slope = feature_slope(k)
-    dk = dk.astype(F32) + dot(v, u, 1, 0)
-    dv = dv.astype(F32) + dot(kf, u, 1, 1)
-    return (dk * k_slope).astype(BF16), dv.astype(BF16)
+def last_body(kf, v, u, dk, dv):
+    cuts = [slice(i, i + DH) for i in range(0, u.shape[0], DH)]
+    dk = dk.astype(F32) + jnp.concatenate([dot(v[:, h], u[h], 1, 0) for h in cuts], 1)
+    dv = dv.astype(F32) + jnp.concatenate([dot(kf[:, h], u[h], 1, 1) for h in cuts], 1)
+    return (dk * jnp.minimum(kf.astype(F32), 1.0)).astype(BF16), dv.astype(BF16)
 
 
 def chunk(ref, at, size, tall):
@@ -203,18 +205,18 @@
     state = jax.ShapeDtypeStruct((width, DH), BF16)
 
     turned = jax.ShapeDtypeStruct((width, rows), BF16)
-    (own,) = stream(own_body, "own", [keys, values], [state], STEP, 2 * DH)
+    (own,) = stream(own_body, "own", [keys, values], [state], STEP, 2 * DH, together=STEP)
     prefix = exclusive_scan(own, n, False)
-    mixed_local, grad_turned, query_feat = stream(
-        pre_body, "pre", [queries, keys, values, grad_out], [turned, turned, wide(BF16)], STEP, 4 * rows
+    mixed_local, grad_turned, query_feat, key_feat = stream(
+        pre_body, "pre", [queries, keys, values, grad_out], [turned, turned, wide(BF16), wide(BF16)], STEP, 4 * rows, (), (2,)
     )
-    (qg,) = stream(fwd_body, "fwd", [query_feat, grad_turned, mixed_local, prefix], [state], STEP, 4 * DH, (3,), together=STEP)
+    (qg,) = stream(fwd_body, "fwd", [query_feat, grad_turned, mixed_local, prefix], [state], STEP, 4 * DH, (0, 3), together=STEP)
     suffix = exclusive_scan(qg, n, True)
     output, grad_q, dk, dv = stream(
-        mid_body, "mid", [queries, keys, values, grad_turned, mixed_local, prefix], [wide(BF16)] * 4, STEP, 10 * rows
+        mid_body, "mid", [queries, key_feat, values, grad_turned, mixed_local, prefix], [wide(BF16)] * 4, STEP, 10 * rows, (), (2,)
     )
     grad_k, grad_v = stream(
-        last_body, "last", [keys, values, suffix, dk, dv], [wide(BF16), wide(BF16)], STEP, 4 * DH, (2,)
+        last_body, "last", [key_feat, values, suffix, dk, dv], [wide(BF16), wide(BF16)], STEP, 4 * DH, (2, 3), together=STEP
     )
     return (output, grad_q, grad_k, grad_v)
 

time: 141 us -> 139 us (0.986)
  Pallas kernels: 45.8 us -> 44.3 us
    pallas_call x5, Pallas kernels: 43.6 us -> 42.2 us  [stream(): pl.pallas_call(functools.partial(stream_kernel, body, step, together, tal...]
where the time goes in v4:
time: 139 us
  blocking collectives  62.9 us (45%)
  Pallas kernels  44.3 us (32%)
  waiting for transfers between devices  24.4 us (18%)
  starting transfers between devices  6.31 us (5%)
    all_to_all x2, blocking collectives, exclusive_scan(): x = lax.all_to_all(state, AXES, 0, 0, tiled=True)  62.9 us
    pallas_call x5, Pallas kernels, stream(): pl.pallas_call(functools.partial(stream_kernel, body, step, together, tal...  42.2 us
    all_to_all x2, waiting for transfers between devices, exclusive_scan(): return lax.all_to_all(y, AXES, 0, 0, tiled=True)  24.4 us
    all_to_all x2, starting transfers between devices, exclusive_scan(): return lax.all_to_all(y, AXES, 0, 0, tiled=True)  6.31 us
  transfers between devices with their start and end apart: 2, of which 2 were waited for; matrix products, arithmetic and copies ran while one was open for 0% of the time, Pallas kernels for 20%

profile of v4, /device:TPU:1, one launch (start us, length us, event | category | flops | bytes accessed | tf_op | source)
XLA Modules:
  0.0 138.6 jit_solution(6602379200592798432)
XLA Ops:
  0.6 3.8 %own.1 = bf16[4096,128]{1,0:T(8,128)(2,1)} custom-call(bf16[256,4096]{1,0:T(8,128)(2,1)} %refs_0_.4, bf16[256,4096]{1,0:T(8,128)(2,1)} %refs_1_.5), custom_call_target="tpu_custom_call" | custom-call | flops 268435456 | bytes 5242880 | tf_op jit(solution)/shard_map/own/pallas_call | solution.py:153
  4.4 33.4 %all_to_all.44 = bf16[32,128,128]{2,1,0:T(8,128)(2,1)S(1)} all-to-all(bf16[32,128,128]{2,1,0:T(8,128)(2,1)} %bitcast.13), channel_id=1, replica_groups=mesh['seq'=8,'head'=4] {'seq','head'}, dimensions={0} | all-to-all | bytes 2097152 | tf_op jit(solution)/shard_map/all_to_all | solution.py:188
  37.8 1.0 scan.2
  38.9 3.2 %all-to-all-start.1 = ((bf16[32,128,128]{2,1,0:T(8,128)(2,1)}), bf16[32,128,128]{2,1,0:T(8,128)(2,1)S(1)}, u32[]{:S(2)}, u32[]{:S(2)}) async-start(bf16[32,128,128]{2,1,0:T(8,128)(2,1)} %bitcast.15), calls=%async_computation.1 | async-start | bytes 2097152 | tf_op jit(solution)/shard_map/all_to_all | solution.py:198
  42.1 6.6 %pre.1 = (bf16[4096,256]{1,0:T(8,128)(2,1)}, bf16[4096,256]{1,0:T(8,128)(2,1)}, bf16[256,4096]{1,0:T(8,128)(2,1)S(1)}, bf16[256,4096]{1,0:T(8,128)(2,1)}) custom-call(bf16[256,4096]{1,0:T(8,128)(2,1)} %refs_0_.5, bf16[256,4096]{1,0:T(8,128)(2,1)} %refs_0_.4, bf16[256,4096]{1,0:T(8,128)(2,1)} %refs_1_.5, bf16[256,4096]{1,0:T(8,128)(2,1)} %refs_3_.1), custom_call_target="tpu_custom_call" | custom-call | flops 1073741824 | bytes 16777216 | tf_op jit(solution)/shard_map/pre/pallas_call | solution.py:153
  48.7 19.7 %all-to-all-done.1 = bf16[32,128,128]{2,1,0:T(8,128)(2,1)S(1)} async-done(((bf16[32,128,128]{2,1,0:T(8,128)(2,1)}), bf16[32,128,128]{2,1,0:T(8,128)(2,1)S(1)}, u32[]{:S(2)}, u32[]{:S(2)}) %all-to-all-start.1) | async-done | bytes 1048608 | tf_op jit(solution)/shard_map/all_to_all | solution.py:198
  68.4 0.0 copy-start
  68.4 5.4 %fwd.1 = bf16[4096,128]{1,0:T(8,128)(2,1)} custom-call(bf16[256,4096]{1,0:T(8,128)(2,1)S(1)} %get-tuple-element.19.refs_0_, bf16[4096,256]{1,0:T(8,128)(2,1)} %get-tuple-element.15.refs_3_.refs_1_, bf16[4096,256]{1,0:T(8,128)(2,1)} %get-tuple-element.16.refs_4_.refs_2_, bf16[4096,128]{1,0:T(8,128)(2,1)S(1)} %bitcast.8), custom_call_target="tpu_custom_call" | custom-call | flops 536870912 | bytes 8388608 | tf_op jit(solution)/shard_map/fwd/pallas_call | solution.py:153
  73.8 0.0 copy-done
  73.8 29.5 %all_to_all.45 = bf16[32,128,128]{2,1,0:T(8,128)(2,1)S(1)} all-to-all(bf16[32,128,128]{2,1,0:T(8,128)(2,1)} %bitcast.16), channel_id=1, replica_groups=mesh['seq'=8,'head'=4] {'seq','head'}, dimensions={0} | all-to-all | bytes 2097152 | tf_op jit(solution)/shard_map/all_to_all | solution.py:188
  103.3 1.1 scan.3
  104.4 3.2 %all-to-all-start.3 = ((bf16[32,128,128]{2,1,0:T(8,128)(2,1)}), bf16[32,128,128]{2,1,0:T(8,128)(2,1)S(1)}, u32[]{:S(2)}, u32[]{:S(2)}) async-start(bf16[32,128,128]{2,1,0:T(8,128)(2,1)} %bitcast.14), calls=%async_computation.3 | async-start | bytes 2097152 | tf_op jit(solution)/shard_map/all_to_all | solution.py:198
  107.5 21.7 %mid.1 = (bf16[256,4096]{1,0:T(8,128)(2,1)}, bf16[256,4096]{1,0:T(8,128)(2,1)}, bf16[256,4096]{1,0:T(8,128)(2,1)S(1)}, bf16[256,4096]{1,0:T(8,128)(2,1)}) custom-call(bf16[256,4096]{1,0:T(8,128)(2,1)} %refs_0_.5, bf16[256,4096]{1,0:T(8,128)(2,1)} %get-tuple-element.14.refs_1_.refs_0_, bf16[256,4096]{1,0:T(8,128)(2,1)} %refs_1_.5, ...), custom_call_target="tpu_custom_call" | custom-call | flops 2684354560 | bytes 19922944 | tf_op jit(solution)/shard_map/mid/pallas_call | solution.py:153
  129.2 4.7 %all-to-all-done.3 = bf16[32,128,128]{2,1,0:T(8,128)(2,1)S(1)} async-done(((bf16[32,128,128]{2,1,0:T(8,128)(2,1)}), bf16[32,128,128]{2,1,0:T(8,128)(2,1)S(1)}, u32[]{:S(2)}, u32[]{:S(2)}) %all-to-all-start.3) | async-done | bytes 1048608 | tf_op jit(solution)/shard_map/all_to_all | solution.py:198
  133.9 4.8 %last.1 = (bf16[256,4096]{1,0:T(8,128)(2,1)}, bf16[256,4096]{1,0:T(8,128)(2,1)}) custom-call(bf16[256,4096]{1,0:T(8,128)(2,1)} %get-tuple-element.14.refs_1_.refs_0_, bf16[256,4096]{1,0:T(8,128)(2,1)} %refs_1_.5, bf16[4096,128]{1,0:T(8,128)(2,1)S(1)} %bitcast.10, bf16[256,4096]{1,0:T(8,128)(2,1)S(1)} %get-tuple-element.20.refs_3_, ...), custom_call_target="tpu_custom_call" | custom-call | flops 536870912 | bytes 13631488 | tf_op jit(solution)/shard_map/last/pallas_call | solution.py:153
Async XLA Ops:
  38.9 29.5 %all-to-all-start.1 = ((bf16[32,128,128]{2,1,0:T(8,128)(2,1)}), bf16[32,128,128]{2,1,0:T(8,128)(2,1)S(1)}, u32[]{:S(2)}, u32[]{:S(2)}) async-start(bf16[32,128,128]{2,1,0:T(8,128)(2,1)} %bitcast.15), calls=%async_computation.1 | async-start | bytes 2097152 | tf_op jit(solution)/shard_map/all_to_all | solution.py:198
  68.4 5.4 %copy-start = (bf16[32,128,128]{2,1,0:T(8,128)(2,1)}, bf16[32,128,128]{2,1,0:T(8,128)(2,1)S(1)}, u32[]{:S(2)}) copy-start(bf16[32,128,128]{2,1,0:T(8,128)(2,1)S(1)} %all-to-all-done.1) | copy-start | bytes 3145732
  104.4 29.5 %all-to-all-start.3 = ((bf16[32,128,128]{2,1,0:T(8,128)(2,1)}), bf16[32,128,128]{2,1,0:T(8,128)(2,1)S(1)}, u32[]{:S(2)}, u32[]{:S(2)}) async-start(bf16[32,128,128]{2,1,0:T(8,128)(2,1)} %bitcast.14), calls=%async_computation.3 | async-start | bytes 2097152 | tf_op jit(solution)/shard_map/all_to_all | solution.py:198

commit v5 on v4

--- a/solution.py
+++ b/solution.py
@@ -109,9 +109,12 @@
             chunk(ins[i], c, size, tall_in[i]), chunk(in_bufs[i], c, size, tall_in[i]), in_sem.at[i, c]
         )
 
-    def put(i, c):
+    span = together * DH
+    groups = step // together
+
+    def put(i, at):
         return pltpu.make_async_copy(
-            chunk(out_bufs[i], c, size, tall_out[i]), chunk(outs[i], c, size, tall_out[i]), out_sem.at[i, c]
+            chunk(out_bufs[i], at, span, tall_out[i]), chunk(outs[i], at, span, tall_out[i]), out_sem.at[i, at]
         )
 
     @pl.loop(0, steps)
@@ -123,19 +126,18 @@
     def _(c):
         for i in moved_in:
             fetch(i, c).wait()
-        span = together * DH
-        for j in range(step // together):
-            at = c * (step // together) + j
+        for j in range(groups):
+            at = c * groups + j
             values = [chunk(in_bufs[i], at, span, tall_in[i])[...] for i in range(ni)]
             for i, value in enumerate(body(*values)):
                 chunk(out_bufs[i], at, span, tall_out[i])[...] = value
+            for i in moved_out:
+                put(i, at).start()
+
+    @pl.loop(0, steps * groups)
+    def _(at):
         for i in moved_out:
-            put(i, c).start()
-
-    @pl.loop(0, steps)
-    def _(c):
-        for i in moved_out:
-            put(i, c).wait()
+            put(i, at).wait()
 
 
 def stream(body, name, args, outs, step, flops, held_in=(), held_out=(), together=1):
@@ -156,7 +158,7 @@
         out_specs=[spec(h) for h in held_out],
         out_shape=[(pltpu.VMEM if h else pltpu.HBM)(o.shape, o.dtype) for o, h in zip(outs, held_out)],
         scratch_shapes=bufs
-        + [pltpu.SemaphoreType.DMA((len(args), steps)), pltpu.SemaphoreType.DMA((len(outs), steps))],
+        + [pltpu.SemaphoreType.DMA((len(args), steps)), pltpu.SemaphoreType.DMA((len(outs), width // DH // together))],
         name=name,
         compiler_params=pltpu.CompilerParams(vmem_limit_bytes=VMEM_LIMIT),
         cost_estimate=pl.CostEstimate(
@@ -167,7 +169,7 @@
 
 def scan_kernel(n, reverse, x_ref, o_ref, buf, sem):
     r = x_ref.shape[0] // n
-    parts = 4 if n % 4 == 0 else 1
+    parts = 8 if n % 8 == 0 else 1
     span = n // parts
     total = jnp.zeros((r, DH), F32)
     copies = []
@@ -191,7 +193,7 @@
         out_shape=pltpu.HBM((rows, DH), BF16),
         in_specs=[pl.BlockSpec(memory_space=pltpu.VMEM)],
         out_specs=pl.BlockSpec(memory_space=pltpu.HBM),
-        scratch_shapes=[pltpu.VMEM((rows, DH), BF16), pltpu.SemaphoreType.DMA((4,))],
+        scratch_shapes=[pltpu.VMEM((rows, DH), BF16), pltpu.SemaphoreType.DMA((8,))],
         name="scan",
         compiler_params=pltpu.CompilerParams(vmem_limit_bytes=VMEM_LIMIT),
     )(pltpu.with_memory_space_constraint(x, pltpu.VMEM))
@@ -205,7 +207,7 @@
     state = jax.ShapeDtypeStruct((width, DH), BF16)
 
     turned = jax.ShapeDtypeStruct((width, rows), BF16)
-    (own,) = stream(own_body, "own", [keys, values], [state], STEP, 2 * DH, together=STEP)
+    (own,) = stream(own_body, "own", [keys, values], [state], STEP, 2 * DH, together=4)
     prefix = exclusive_scan(own, n, False)
     mixed_local, grad_turned, query_feat, key_feat = stream(
         pre_body, "pre", [queries, keys, values, grad_out], [turned, turned, wide(BF16), wide(BF16)], STEP, 4 * rows, (), (2,)
@@ -216,7 +218,7 @@
         mid_body, "mid", [queries, key_feat, values, grad_turned, mixed_local, prefix], [wide(BF16)] * 4, STEP, 10 * rows, (), (2,)
     )
     grad_k, grad_v = stream(
-        last_body, "last", [key_feat, values, suffix, dk, dv], [wide(BF16), wide(BF16)], STEP, 4 * DH, (2, 3), together=STEP
+        last_body, "last", [key_feat, values, suffix, dk, dv], [wide(BF16), wide(BF16)], STEP, 4 * DH, (2, 3), together=4
     )
     return (output, grad_q, grad_k, grad_v)
 

time: 139 us -> 139 us (level)
  Pallas kernels: 44.3 us -> 47.4 us
  waiting for transfers between devices: 24.4 us -> 21.5 us
    pallas_call x5, Pallas kernels: 42.2 us -> 45.3 us  [stream(): pl.pallas_call(functools.partial(stream_kernel, body, step, together, tal...]
    all_to_all x2, waiting for transfers between devices: 24.4 us -> 21.5 us  [exclusive_scan(): return lax.all_to_all(y, AXES, 0, 0, tiled=True)]
  transfers between devices with their start and end apart: 2 -> 2, of which waited for: 2 -> 2; matrix products, arithmetic and copies ran while one was open for 0% -> 0% of each run, Pallas kernels for 20% -> 22%
where the time goes in v5:
time: 139 us
  blocking collectives  62.9 us (45%)
  Pallas kernels  47.4 us (34%)
  waiting for transfers between devices  21.5 us (15%)
  starting transfers between devices  6.31 us (5%)
    all_to_all x2, blocking collectives, exclusive_scan(): x = lax.all_to_all(state, AXES, 0, 0, tiled=True)  62.9 us
    pallas_call x5, Pallas kernels, stream(): pl.pallas_call(functools.partial(stream_kernel, body, step, together, tal...  45.3 us
    all_to_all x2, waiting for transfers between devices, exclusive_scan(): return lax.all_to_all(y, AXES, 0, 0, tiled=True)  21.5 us
    all_to_all x2, starting transfers between devices, exclusive_scan(): return lax.all_to_all(y, AXES, 0, 0, tiled=True)  6.31 us
  transfers between devices with their start and end apart: 2, of which 2 were waited for; matrix products, arithmetic and copies ran while one was open for 0% of the time, Pallas kernels for 22%

profile of v5, /device:TPU:1, one launch (start us, length us, event | category | flops | bytes accessed | tf_op | source)
XLA Modules:
  0.0 138.9 jit_solution(7503277322762970537)
XLA Ops:
  0.6 3.8 %own.1 = bf16[4096,128]{1,0:T(8,128)(2,1)} custom-call(bf16[256,4096]{1,0:T(8,128)(2,1)} %refs_0_.4, bf16[256,4096]{1,0:T(8,128)(2,1)} %refs_1_.5), custom_call_target="tpu_custom_call" | custom-call | flops 268435456 | bytes 5242880 | tf_op jit(solution)/shard_map/own/pallas_call | solution.py:155
  4.4 33.5 %all_to_all.44 = bf16[32,128,128]{2,1,0:T(8,128)(2,1)S(1)} all-to-all(bf16[32,128,128]{2,1,0:T(8,128)(2,1)} %bitcast.13), channel_id=1, replica_groups=mesh['seq'=8,'head'=4] {'seq','head'}, dimensions={0} | all-to-all | bytes 2097152 | tf_op jit(solution)/shard_map/all_to_all | solution.py:190
  37.8 1.0 scan.2
  38.9 3.2 %all-to-all-start.1 = ((bf16[32,128,128]{2,1,0:T(8,128)(2,1)}), bf16[32,128,128]{2,1,0:T(8,128)(2,1)S(1)}, u32[]{:S(2)}, u32[]{:S(2)}) async-start(bf16[32,128,128]{2,1,0:T(8,128)(2,1)} %bitcast.15), calls=%async_computation.1 | async-start | bytes 2097152 | tf_op jit(solution)/shard_map/all_to_all | solution.py:200
  42.1 7.7 %pre.1 = (bf16[4096,256]{1,0:T(8,128)(2,1)}, bf16[4096,256]{1,0:T(8,128)(2,1)}, bf16[256,4096]{1,0:T(8,128)(2,1)S(1)}, bf16[256,4096]{1,0:T(8,128)(2,1)}) custom-call(bf16[256,4096]{1,0:T(8,128)(2,1)} %refs_0_.5, bf16[256,4096]{1,0:T(8,128)(2,1)} %refs_0_.4, bf16[256,4096]{1,0:T(8,128)(2,1)} %refs_1_.5, bf16[256,4096]{1,0:T(8,128)(2,1)} %refs_3_.1), custom_call_target="tpu_custom_call" | custom-call | flops 1073741824 | bytes 16777216 | tf_op jit(solution)/shard_map/pre/pallas_call | solution.py:155
  49.7 18.6 %all-to-all-done.1 = bf16[32,128,128]{2,1,0:T(8,128)(2,1)S(1)} async-done(((bf16[32,128,128]{2,1,0:T(8,128)(2,1)}), bf16[32,128,128]{2,1,0:T(8,128)(2,1)S(1)}, u32[]{:S(2)}, u32[]{:S(2)}) %all-to-all-start.1) | async-done | bytes 1048608 | tf_op jit(solution)/shard_map/all_to_all | solution.py:200
  68.4 0.0 copy-start
  68.4 5.4 %fwd.1 = bf16[4096,128]{1,0:T(8,128)(2,1)} custom-call(bf16[256,4096]{1,0:T(8,128)(2,1)S(1)} %get-tuple-element.19.refs_0_, bf16[4096,256]{1,0:T(8,128)(2,1)} %get-tuple-element.15.refs_3_.refs_1_, bf16[4096,256]{1,0:T(8,128)(2,1)} %get-tuple-element.16.refs_4_.refs_2_, bf16[4096,128]{1,0:T(8,128)(2,1)S(1)} %bitcast.8), custom_call_target="tpu_custom_call" | custom-call | flops 536870912 | bytes 8388608 | tf_op jit(solution)/shard_map/fwd/pallas_call | solution.py:155
  73.8 0.0 copy-done
  73.8 29.5 %all_to_all.45 = bf16[32,128,128]{2,1,0:T(8,128)(2,1)S(1)} all-to-all(bf16[32,128,128]{2,1,0:T(8,128)(2,1)} %bitcast.16), channel_id=1, replica_groups=mesh['seq'=8,'head'=4] {'seq','head'}, dimensions={0} | all-to-all | bytes 2097152 | tf_op jit(solution)/shard_map/all_to_all | solution.py:190
  103.3 1.1 scan.3
  104.4 3.2 %all-to-all-start.3 = ((bf16[32,128,128]{2,1,0:T(8,128)(2,1)}), bf16[32,128,128]{2,1,0:T(8,128)(2,1)S(1)}, u32[]{:S(2)}, u32[]{:S(2)}) async-start(bf16[32,128,128]{2,1,0:T(8,128)(2,1)} %bitcast.14), calls=%async_computation.3 | async-start | bytes 2097152 | tf_op jit(solution)/shard_map/all_to_all | solution.py:200
  107.6 23.4 %mid.1 = (bf16[256,4096]{1,0:T(8,128)(2,1)}, bf16[256,4096]{1,0:T(8,128)(2,1)}, bf16[256,4096]{1,0:T(8,128)(2,1)S(1)}, bf16[256,4096]{1,0:T(8,128)(2,1)}) custom-call(bf16[256,4096]{1,0:T(8,128)(2,1)} %refs_0_.5, bf16[256,4096]{1,0:T(8,128)(2,1)} %get-tuple-element.14.refs_1_.refs_0_, bf16[256,4096]{1,0:T(8,128)(2,1)} %refs_1_.5, ...), custom_call_target="tpu_custom_call" | custom-call | flops 2684354560 | bytes 19922944 | tf_op jit(solution)/shard_map/mid/pallas_call | solution.py:155
  131.0 2.9 %all-to-all-done.3 = bf16[32,128,128]{2,1,0:T(8,128)(2,1)S(1)} async-done(((bf16[32,128,128]{2,1,0:T(8,128)(2,1)}), bf16[32,128,128]{2,1,0:T(8,128)(2,1)S(1)}, u32[]{:S(2)}, u32[]{:S(2)}) %all-to-all-start.3) | async-done | bytes 1048608 | tf_op jit(solution)/shard_map/all_to_all | solution.py:200
  133.9 5.0 %last.1 = (bf16[256,4096]{1,0:T(8,128)(2,1)}, bf16[256,4096]{1,0:T(8,128)(2,1)}) custom-call(bf16[256,4096]{1,0:T(8,128)(2,1)} %get-tuple-element.14.refs_1_.refs_0_, bf16[256,4096]{1,0:T(8,128)(2,1)} %refs_1_.5, bf16[4096,128]{1,0:T(8,128)(2,1)S(1)} %bitcast.10, bf16[256,4096]{1,0:T(8,128)(2,1)S(1)} %get-tuple-element.20.refs_3_, ...), custom_call_target="tpu_custom_call" | custom-call | flops 536870912 | bytes 13631488 | tf_op jit(solution)/shard_map/last/pallas_call | solution.py:155
Async XLA Ops:
  38.9 29.5 %all-to-all-start.1 = ((bf16[32,128,128]{2,1,0:T(8,128)(2,1)}), bf16[32,128,128]{2,1,0:T(8,128)(2,1)S(1)}, u32[]{:S(2)}, u32[]{:S(2)}) async-start(bf16[32,128,128]{2,1,0:T(8,128)(2,1)} %bitcast.15), calls=%async_computation.1 | async-start | bytes 2097152 | tf_op jit(solution)/shard_map/all_to_all | solution.py:200
  68.4 5.4 %copy-start = (bf16[32,128,128]{2,1,0:T(8,128)(2,1)}, bf16[32,128,128]{2,1,0:T(8,128)(2,1)S(1)}, u32[]{:S(2)}) copy-start(bf16[32,128,128]{2,1,0:T(8,128)(2,1)S(1)} %all-to-all-done.1) | copy-start | bytes 3145732
  104.4 29.5 %all-to-all-start.3 = ((bf16[32,128,128]{2,1,0:T(8,128)(2,1)}), bf16[32,128,128]{2,1,0:T(8,128)(2,1)S(1)}, u32[]{:S(2)}, u32[]{:S(2)}) async-start(bf16[32,128,128]{2,1,0:T(8,128)(2,1)} %bitcast.14), calls=%async_computation.3 | async-start | bytes 2097152 | tf_op jit(solution)/shard_map/all_to_all | solution.py:200
